TPU v7x, 512 devices: a whole 4x4x16 slice. The times are simulated.
512 devices in a mesh: wide: 32 (over z, core), narrow: 16 (over y, x).
Axes of the slice: x: 4, y: 4, z: 16, core: 2. Of those that a mesh axis runs over, the one named last changes fastest.
Arguments:
- hidden: bfloat16 [2048, 2048], P('wide'), may hold values from -6 to 6
- attn_gain: float32 [2048], replicated, may hold values from 0.1 to 1.9
- expert_gain: float32 [2048], replicated, may hold values from 0.1 to 1.9
- query_weight: bfloat16 [2048, 2048], P('wide', 'narrow'), may hold values from -0.125 to 0.125
- key_weight: bfloat16 [2048, 2048], P('wide', 'narrow'), may hold values from -0.125 to 0.125
- value_weight: bfloat16 [2048, 2048], P('wide', 'narrow'), may hold values from -0.125 to 0.125
- output_weight: bfloat16 [2048, 2048], P('wide', 'narrow'), may hold values from -0.125 to 0.125
- router_weight: bfloat16 [2048, 64], replicated, may hold values from -0.125 to 0.125
- gate_weight: bfloat16 [64, 2048, 1024], P('wide', None, 'narrow'), may hold values from -0.125 to 0.125
- up_weight: bfloat16 [64, 2048, 1024], P('wide', None, 'narrow'), may hold values from -0.125 to 0.125
- down_weight: bfloat16 [64, 1024, 2048], P('wide', 'narrow'), may hold values from -0.1875 to 0.1875
- prefix_keys: bfloat16 [256, 8, 2048], P('wide', None, 'narrow'), may hold values from -6 to 6
- prefix_values: bfloat16 [256, 8, 2048], P('wide', None, 'narrow'), may hold values from -6 to 6
- cache_keys: bfloat16 [32, 1024, 2048], P('wide', None, 'narrow'), may hold values from -256 to 256
- cache_values: bfloat16 [32, 1024, 2048], P('wide', None, 'narrow'), may hold values from -6 to 6
- parents: int32 [32, 64], P('wide'), may hold values from 0 to 62, as said below
- cache_lengths: int32 [32], P('wide'), may hold values from 1 to 960, 15360 in all
- group_ids: int32 [32], replicated, may hold values from 0 to 7
- expert_ids: int32 [2048, 8], P('wide'), may hold values from 0 to 63, all different within a row; in each aligned block of 64 rows (0 to 63, 64 to 127, ...) at most 9 rows name the same one
- accepted: int32 [32], P('wide'), may hold values from 0 to 63
Outputs:
- layer_out: bfloat16 [2048, 2048], P('wide', 'narrow')
- new_keys: bfloat16 [32, 1024, 2048], P('wide', None, 'narrow')
- new_values: bfloat16 [32, 1024, 2048], P('wide', None, 'narrow')
Inputs may be any that keep to these rules, and one draw needn't show every extreme that they name: `parents`: node 0 of each tree is the root and its own parent; node i > 0 has its parent among nodes max(0, i - 4) to i - 1; the parent of node 63 is node 62. `expert_ids`: the 8 experts of a token differ; among the tokens of one index of wide no expert is named more than 9 times, a bound that some block reaches in some of them.
All inputs are finite; a program needn't handle non-finite values. No bound on the sum of `cache_lengths` on one device may be relied on, other than what follows from the above.
Results may differ from a plain program's by a relative error of at most 0.01.
The roundings to bfloat16 on the way count: a program that leaves them out, or rounds other values in their place, can miss the bound.
Values may be sent and summed in bfloat16 or wider, within the bound.
A program may use at most 64 MiB of HBM per device.

v0:
```python
import math

import jax
import jax.numpy as jnp
from jax import lax
from jax.sharding import PartitionSpec as P

HD = 128
E = 64
SINK = 4
WIN = 512
CAP = 9


norm_eps = 1e-06


def rms_scale(rows, row_gain):
    widened = rows.astype(jnp.float32)
    power_mean = jnp.mean(widened * widened, axis=-1, keepdims=True)
    return (widened * lax.rsqrt(power_mean + norm_eps) * row_gain).astype(jnp.bfloat16)


def tree_links(parents):
    tree_size = parents.shape[-1]
    node_ids = jnp.arange(tree_size, dtype=jnp.int32)
    linked = (node_ids[:, None] == node_ids[None, :]) | (parents[..., :, None] == node_ids)
    jumper = parents
    for doubling in range(tree_size.bit_length()):
        hop_table = (jumper[..., :, None] == node_ids).astype(jnp.float32)
        through = jnp.einsum(
            "...ij,...jk->...ik",
            hop_table,
            linked.astype(jnp.float32),
            precision=lax.Precision.HIGHEST,
        )
        linked = linked | (through > 0.5)
        jumper = jnp.take_along_axis(jumper, jumper, axis=-1)
    depths = jnp.sum(linked.astype(jnp.int32), axis=-1) - 1
    return (linked, depths)


def body(
    hidden,
    attn_gain,
    expert_gain,
    query_weight,
    key_weight,
    value_weight,
    output_weight,
    router_weight,
    gate_weight,
    up_weight,
    down_weight,
    prefix_keys,
    prefix_values,
    cache_keys,
    cache_values,
    parents,
    cache_lengths,
    group_ids,
    expert_ids,
    accepted,
):
    tok_count, model_width = hidden.shape
    req_count, tree_size = parents.shape
    cache_size = cache_keys.shape[1]
    local_width = query_weight.shape[1]
    head_size = HD
    head_count = local_width // head_size
    group_count = prefix_keys.shape[1]
    narrow_count = lax.axis_size("narrow")
    wide_count = lax.axis_size("wide")
    slice_width = model_width // narrow_count
    narrow_pos = lax.axis_index("narrow")
    wide_pos = lax.axis_index("wide")
    scale_factor = 1.0 / math.sqrt(head_size)
    normed = rms_scale(hidden, attn_gain)
    own_groups = lax.dynamic_slice_in_dim(group_ids, wide_pos * req_count, req_count)
    gathered = (
        lax.all_gather(query_weight, "wide", axis=0, tiled=True),
        lax.all_gather(key_weight, "wide", axis=0, tiled=True),
        lax.all_gather(value_weight, "wide", axis=0, tiled=True),
        lax.all_gather(output_weight, "wide", axis=0, tiled=True),
        lax.all_gather(prefix_keys, "wide", axis=0, tiled=True),
        lax.all_gather(prefix_values, "wide", axis=0, tiled=True),
    )
    query_full, key_full, value_full, output_full, shared_keys, shared_values = gathered
    prefix_len = shared_keys.shape[0]
    group_keys = jnp.take(
        shared_keys.reshape(prefix_len, group_count, head_count, head_size), own_groups, axis=1
    )
    group_values = jnp.take(
        shared_values.reshape(prefix_len, group_count, head_count, head_size), own_groups, axis=1
    )
    queries = jnp.dot(normed, query_full, preferred_element_type=jnp.float32).astype(jnp.bfloat16)
    keys_new = jnp.dot(normed, key_full, preferred_element_type=jnp.float32).astype(jnp.bfloat16)
    values_new = jnp.dot(normed, value_full, preferred_element_type=jnp.float32).astype(
        jnp.bfloat16
    )
    block_shape = (req_count, tree_size, head_count, head_size)
    query_blocks = queries.reshape(block_shape)
    key_blocks = keys_new.reshape(block_shape)
    value_blocks = values_new.reshape(block_shape)
    own_keys = cache_keys.reshape(req_count, cache_size, head_count, head_size)
    own_values = cache_values.reshape(req_count, cache_size, head_count, head_size)
    slot_ids = jnp.arange(cache_size, dtype=jnp.int32)
    lengths = cache_lengths[:, None]
    cache_mask = (slot_ids < lengths) & ((slot_ids < SINK) | (slot_ids >= lengths - WIN))
    ancestry, depths = tree_links(parents)
    cache_allowed = cache_mask[:, None, None, :]
    tree_allowed = ancestry[:, None, :, :]
    prefix_scores = (
        jnp.einsum("rqhd,prhd->rhqp", query_blocks, group_keys, preferred_element_type=jnp.float32)
        * scale_factor
    )
    cache_scores = (
        jnp.einsum("rqhd,rkhd->rhqk", query_blocks, own_keys, preferred_element_type=jnp.float32)
        * scale_factor
    )
    tree_scores = (
        jnp.einsum("rqhd,rkhd->rhqk", query_blocks, key_blocks, preferred_element_type=jnp.float32)
        * scale_factor
    )
    row_top = jnp.maximum(
        jnp.max(prefix_scores, axis=-1),
        jnp.maximum(
            jnp.max(jnp.where(cache_allowed, cache_scores, -jnp.inf), axis=-1),
            jnp.max(jnp.where(tree_allowed, tree_scores, -jnp.inf), axis=-1),
        ),
    )[..., None]
    prefix_weights = jnp.exp(prefix_scores - row_top)
    cache_weights = jnp.where(cache_allowed, jnp.exp(cache_scores - row_top), 0.0)
    tree_weights = jnp.where(tree_allowed, jnp.exp(tree_scores - row_top), 0.0)
    row_total = (
        jnp.sum(prefix_weights, axis=-1)
        + jnp.sum(cache_weights, axis=-1)
        + jnp.sum(tree_weights, axis=-1)
    )
    weighted = jnp.einsum(
        "rhqp,prhd->rqhd",
        prefix_weights.astype(jnp.bfloat16),
        group_values,
        preferred_element_type=jnp.float32,
    )
    weighted = weighted + jnp.einsum(
        "rhqk,rkhd->rqhd",
        cache_weights.astype(jnp.bfloat16),
        own_values,
        preferred_element_type=jnp.float32,
    )
    weighted = weighted + jnp.einsum(
        "rhqk,rkhd->rqhd",
        tree_weights.astype(jnp.bfloat16),
        value_blocks,
        preferred_element_type=jnp.float32,
    )
    attended = (
        (weighted / jnp.transpose(row_total, (0, 2, 1))[..., None])
        .astype(jnp.bfloat16)
        .reshape(tok_count, local_width)
    )
    partial_value = lax.dot_general(
        attended, output_full, (((1,), (1,)), ((), ())), preferred_element_type=jnp.float32
    )
    summed = lax.psum(partial_value, "narrow")
    mixed = (hidden.astype(jnp.float32) + summed).astype(jnp.bfloat16)
    mixed_part = lax.dynamic_slice_in_dim(mixed, narrow_pos * slice_width, slice_width, 1)
    normed_moe = rms_scale(mixed, expert_gain)
    logits = jnp.dot(normed_moe, router_weight, preferred_element_type=jnp.float32)
    expert_range = jnp.arange(E, dtype=jnp.int32)
    top_count = expert_ids.shape[1]
    matches = expert_ids[:, :, None] == expert_range
    chosen = jnp.sum(jnp.where(matches, logits[:, None, :], 0.0), axis=-1)
    shares = jax.nn.softmax(chosen, axis=-1)
    flat_experts = expert_ids.reshape(-1)
    expert_table = (flat_experts[:, None] == expert_range).astype(jnp.int32)
    earlier = jnp.cumsum(expert_table, axis=0) - expert_table
    slot_ranks = jnp.sum(earlier * expert_table, axis=1)
    targets = flat_experts * CAP + slot_ranks
    repeated = jnp.broadcast_to(
        normed_moe[:, None, :], (tok_count, top_count, model_width)
    ).reshape(tok_count * top_count, model_width)
    exp_local = gate_weight.shape[0]
    send_rows = jnp.zeros((E * CAP, model_width), jnp.bfloat16).at[targets].set(repeated)
    send_rows = send_rows.reshape(wide_count, exp_local, CAP, model_width)
    routed = lax.all_to_all(send_rows, "wide", split_axis=0, concat_axis=0, tiled=True)
    gate_out = jnp.einsum("secd,edf->secf", routed, gate_weight, preferred_element_type=jnp.float32)
    up_out = jnp.einsum("secd,edf->secf", routed, up_weight, preferred_element_type=jnp.float32)
    activated = (jax.nn.silu(gate_out) * up_out).astype(jnp.bfloat16)
    produced = jnp.einsum(
        "secf,efd->secd", activated, down_weight, preferred_element_type=jnp.float32
    ).astype(jnp.bfloat16)
    returned = lax.all_to_all(produced, "wide", split_axis=0, concat_axis=0, tiled=True)
    fetched = returned.reshape(E * CAP, model_width)[targets].reshape(
        tok_count, top_count, model_width
    )
    partial_moe = jnp.sum(shares[:, :, None] * fetched.astype(jnp.float32), axis=1)
    moe_part = lax.psum_scatter(partial_moe, "narrow", scatter_dimension=1, tiled=True)
    layer_out = (mixed_part.astype(jnp.float32) + moe_part).astype(jnp.bfloat16)
    on_path = jnp.take_along_axis(ancestry, accepted[:, None, None], axis=1)[:, 0, :]
    slots = jnp.where(on_path, cache_lengths[:, None] + depths, cache_size)
    request_rows = jnp.broadcast_to(
        jnp.arange(req_count, dtype=jnp.int32)[:, None], (req_count, tree_size)
    )
    new_keys = cache_keys.at[request_rows, slots].set(
        keys_new.reshape(req_count, tree_size, local_width), mode="drop"
    )
    new_values = cache_values.at[request_rows, slots].set(
        values_new.reshape(req_count, tree_size, local_width), mode="drop"
    )
    return (layer_out, new_keys, new_values)


def solution(mesh):
    in_specs = (
        P("wide", None),
        P(),
        P(),
        P("wide", "narrow"),
        P("wide", "narrow"),
        P("wide", "narrow"),
        P("wide", "narrow"),
        P(),
        P("wide", None, "narrow"),
        P("wide", None, "narrow"),
        P("wide", "narrow", None),
        P("wide", None, "narrow"),
        P("wide", None, "narrow"),
        P("wide", None, "narrow"),
        P("wide", None, "narrow"),
        P("wide", None),
        P("wide"),
        P(),
        P("wide", None),
        P("wide"),
    )
    out_specs = (P("wide", "narrow"), P("wide", None, "narrow"), P("wide", None, "narrow"))
    return jax.shard_map(body, mesh=mesh, in_specs=in_specs, out_specs=out_specs, check_vma=False)
```

profile of v0, /device:TPU:1, one launch (start us, length us, event | category | flops | bytes accessed | tf_op | source)
XLA Modules:
  0.0 688.9 jit_solution(3292197298421425880)
XLA Ops:
  7.2 1.0 copy.120
  8.2 1.1 copy.121
  9.9 1.2 dynamic_slice.6
  13.1 0.7 fusion.116
  13.8 1.1 fusion.39
  14.9 1.0 fusion.30
  15.9 1.4 gather_fusion.1
  17.3 0.7 fusion.117
  18.0 0.8 gather_fusion.2
  18.9 0.8 gather_fusion.3
  19.7 0.8 gather_fusion.4
  20.5 0.8 gather_fusion.5
  21.3 0.8 gather_fusion.6
  23.1 39.0 %all_gather.18 = bf16[256,8,128]{2,0,1:T(8,128)(2,1)S(1)} all-gather(bf16[8,8,128]{2,0,1:T(8,128)(2,1)S(1)} %copy.59), channel_id=1, replica_groups=mesh['wide'=32,'narrow'=16] {'wide'}, dimensions={0}, use_global_device_ids=true | all-gather | bytes 540672 | tf_op jit(solution)/shard_map/all_gather | solution.py:86
  62.1 28.5 %all_gather.20 = bf16[256,8,128]{2,0,1:T(8,128)(2,1)S(1)} all-gather(bf16[8,8,128]{2,0,1:T(8,128)(2,1)S(1)} %copy.60), channel_id=1, replica_groups=mesh['wide'=32,'narrow'=16] {'wide'}, dimensions={0}, use_global_device_ids=true | all-gather | bytes 540672 | tf_op jit(solution)/shard_map/all_gather | solution.py:85
  90.6 30.0 %all_gather.19 = bf16[2048,128]{1,0:T(8,128)(2,1)S(1)} all-gather(bf16[64,128]{1,0:T(8,128)(2,1)S(1)} %copy-done.7), channel_id=1, replica_groups=mesh['wide'=32,'narrow'=16] {'wide'}, dimensions={0}, use_global_device_ids=true | all-gather | bytes 540672 | tf_op jit(solution)/shard_map/all_gather | solution.py:81
  120.6 28.5 %all_gather.21 = bf16[2048,128]{1,0:T(8,128)(2,1)S(1)} all-gather(bf16[64,128]{1,0:T(8,128)(2,1)S(1)} %copy-done.8), channel_id=1, replica_groups=mesh['wide'=32,'narrow'=16] {'wide'}, dimensions={0}, use_global_device_ids=true | all-gather | bytes 540672 | tf_op jit(solution)/shard_map/all_gather | solution.py:82
  149.1 0.3 convolution_convert_fusion.3
  149.4 0.3 convolution_convert_fusion.2
  149.8 0.3 select_reduce_fusion.1
  150.4 0.3 select_reduce_fusion.2
  151.6 29.9 %all_gather.22 = bf16[2048,128]{1,0:T(8,128)(2,1)S(1)} all-gather(bf16[64,128]{1,0:T(8,128)(2,1)S(1)} %copy-done.9), channel_id=1, replica_groups=mesh['wide'=32,'narrow'=16] {'wide'}, dimensions={0}, use_global_device_ids=true | all-gather | bytes 540672 | tf_op jit(solution)/shard_map/all_gather | solution.py:83
  181.4 0.3 convolution_convert_fusion.1
  181.7 28.5 %all_gather.23 = bf16[2048,128]{1,0:T(8,128)(2,1)S(1)} all-gather(bf16[64,128]{1,0:T(8,128)(2,1)S(1)} %copy-done.10), channel_id=1, replica_groups=mesh['wide'=32,'narrow'=16] {'wide'}, dimensions={0}, use_global_device_ids=true | all-gather | bytes 540672 | tf_op jit(solution)/shard_map/all_gather | solution.py:84
  210.5 1.3 fusion.35
  212.3 1.2 reduce-window.6
  213.9 108.8 %all-reduce.3.cloned.1.call-done = f32[64,2048]{1,0:T(8,128)} async-done(((f32[64,2048]{1,0:T(8,128)}), f32[64,2048]{1,0:T(8,128)}) %all-reduce.3.cloned.1.call-update) | async-done | bytes 524304 | tf_op jit(solution)/shard_map/psum | solution.py:166
  322.7 1.2 fusion.36
  324.1 0.5 copy-done.5
  324.6 4.5 scatter_custom_fusion
  329.1 2.8 reshape.738
  331.9 4.8 copy.67
  336.8 126.7 %all_to_all.10 = bf16[32,2,9,2048]{3,1,2,0:T(2,128)(2,1)S(1)} all-to-all(bf16[32,2,9,2048]{3,1,2,0:T(2,128)(2,1)S(1)} %copy.67), channel_id=1, replica_groups=mesh['wide'=32,'narrow'=16] {'wide'}, dimensions={0} | all-to-all | bytes 4718592 | tf_op jit(solution)/shard_map/all_to_all | solution.py:187
  463.5 1.6 fusion.9
  465.0 4.1 fusion.1
  469.1 5.5 copy.70
  474.6 4.2 all-to-all-start.1
  478.7 0.3 reduce-scatter.2.cloned.1.call-start
  479.0 1.2 fusion.127
  480.8 107.5 %all-to-all-done.1 = bf16[32,2,9,2048]{3,1,2,0:T(2,128)(2,1)S(1)} async-done(((bf16[32,2,9,2048]{3,1,2,0:T(2,128)(2,1)}), bf16[32,2,9,2048]{3,1,2,0:T(2,128)(2,1)S(1)}, u32[]{:S(2)}, u32[]{:S(2)}) %all-to-all-start.1) | async-done | bytes 2359328 | tf_op jit(solution)/shard_map/all_to_all | solution.py:194
  588.4 3.3 copy.71
  591.7 3.4 reshape.739
  595.1 3.3 gather_fusion
  598.4 4.2 fusion
  603.5 0.9 scatter_fusion
  604.5 0.9 scatter_fusion.1
  605.4 75.3 %reduce-scatter.2.cloned.1.call-done = f32[64,128]{1,0:T(8,128)} async-done(((f32[64,2048]{1,0:T(8,128)}), f32[64,128]{1,0:T(8,128)}) %reduce-scatter.2.cloned.1.call-update) | async-done | bytes 32784 | tf_op jit(solution)/shard_map/reduce_scatter | solution.py:199
  680.7 1.4 add_convert_fusion
  (88 shorter events, 4.4 us)
Async XLA Ops:
  7.2 457.9 %copy-start = (bf16[2,64,2048]{2,1,0:T(8,128)(2,1)S(1)}, bf16[2,64,2048]{2,1,0:T(8,128)(2,1)}, u32[]{:S(2)}) copy-start(bf16[2,64,2048]{2,1,0:T(8,128)(2,1)} %param.34) | copy-start | bytes 1572868
  7.2 315.5 %all-reduce.3.cloned.1.call-start = ((), (), s32[]{:S(2)}) async-start(), calls=%async_computation.3 | async-start | bytes 1048576 | tf_op jit(solution)/shard_map/psum | solution.py:166
  8.2 141.6 %copy-start.2 = (bf16[1,1024,128]{2,1,0:T(8,128)(2,1)}, bf16[1,1024,128]{2,1,0:T(8,128)(2,1)S(1)}, u32[]{:S(2)}) copy-start(bf16[1,1024,128]{2,1,0:T(8,128)(2,1)S(1)} %copy.120) | copy-start | bytes 786436
  8.2 14.8 %copy-start.12 = (bf16[8,8,128]{2,1,0:T(8,128)(2,1)S(1)}, bf16[8,8,128]{2,1,0:T(8,128)(2,1)}, u32[]{:S(2)}) copy-start(bf16[8,8,128]{2,1,0:T(8,128)(2,1)} %param.35) | copy-start | bytes 49156
  8.2 14.8 %copy-start.13 = (bf16[8,8,128]{2,1,0:T(8,128)(2,1)S(1)}, bf16[8,8,128]{2,1,0:T(8,128)(2,1)}, u32[]{:S(2)}) copy-start(bf16[8,8,128]{2,1,0:T(8,128)(2,1)} %param.36) | copy-start | bytes 49156
  15.9 74.7 %copy-start.7 = (bf16[64,128]{1,0:T(8,128)(2,1)S(1)}, bf16[64,128]{1,0:T(8,128)(2,1)}, u32[]{:S(2)}) copy-start(bf16[64,128]{1,0:T(8,128)(2,1)} %param.27) | copy-start | bytes 49156
  18.0 102.5 %copy-start.8 = (bf16[64,128]{1,0:T(8,128)(2,1)S(1)}, bf16[64,128]{1,0:T(8,128)(2,1)}, u32[]{:S(2)}) copy-start(bf16[64,128]{1,0:T(8,128)(2,1)} %param.28) | copy-start | bytes 49156
  18.8 130.2 %copy-start.6 = (bf16[64,2048]{1,0:T(8,128)(2,1)S(1)}, bf16[64,2048]{1,0:T(8,128)(2,1)}, u32[]{:S(2)}) copy-start(bf16[64,2048]{1,0:T(8,128)(2,1)} %param.24) | copy-start | bytes 786436
  18.8 130.2 %copy-start.16 = (f32[2048]{0:T(1024)S(1)}, f32[2048]{0:T(1024)}, u32[]{:S(2)}) copy-start(f32[2048]{0:T(1024)} %param.25) | copy-start | bytes 24580
  90.6 61.0 %copy-start.9 = (bf16[64,128]{1,0:T(8,128)(2,1)S(1)}, bf16[64,128]{1,0:T(8,128)(2,1)}, u32[]{:S(2)}) copy-start(bf16[64,128]{1,0:T(8,128)(2,1)} %param.29) | copy-start | bytes 49156
  149.1 32.6 %copy-start.10 = (bf16[64,128]{1,0:T(8,128)(2,1)S(1)}, bf16[64,128]{1,0:T(8,128)(2,1)}, u32[]{:S(2)}) copy-start(bf16[64,128]{1,0:T(8,128)(2,1)} %param.30) | copy-start | bytes 49156
  150.7 61.1 %copy-start.11 = (s32[64,8]{0,1:T(8,128)S(1)}, s32[64,8]{0,1:T(8,128)}, u32[]{:S(2)}) copy-start(s32[64,8]{0,1:T(8,128)} %param.42) | copy-start | bytes 6148
  181.7 142.2 %copy-start.14 = (f32[2048]{0:T(1024)S(1)}, f32[2048]{0:T(1024)}, u32[]{:S(2)}) copy-start(f32[2048]{0:T(1024)} %param.26) | copy-start | bytes 24580
  323.9 0.7 copy-start.5
  336.8 126.7 %copy-start.15 = (bf16[2,2048,64]{1,2,0:T(8,128)(2,1)S(1)}, bf16[2,2048,64]{1,2,0:T(8,128)(2,1)}, u32[]{:S(2)}) copy-start(bf16[2,2048,64]{1,2,0:T(8,128)(2,1)} %param.32) | copy-start | bytes 1572868
  474.6 113.8 %all-to-all-start.1 = ((bf16[32,2,9,2048]{3,1,2,0:T(2,128)(2,1)}), bf16[32,2,9,2048]{3,1,2,0:T(2,128)(2,1)S(1)}, u32[]{:S(2)}, u32[]{:S(2)}) async-start(bf16[32,2,9,2048]{3,1,2,0:T(2,128)(2,1)} %copy.70), calls=%async_computation.1 | async-start | bytes 4718592 | tf_op jit(solution)/shard_map/all_to_all | solution.py:194
  478.7 202.0 %reduce-scatter.2.cloned.1.call-start = ((), (), s32[]{:S(2)}) async-start(), calls=%async_computation.4 | async-start | bytes 557056 | tf_op jit(solution)/shard_map/reduce_scatter | solution.py:199
  598.4 5.1 copy-start.3
  604.5 77.6 %copy-start.4 = (bf16[1024,128]{1,0:T(8,128)(2,1)}, bf16[1024,128]{1,0:T(8,128)(2,1)S(1)}, u32[]{:S(2)}) copy-start(bf16[1024,128]{1,0:T(8,128)(2,1)S(1)} %scatter_fusion) | copy-start | bytes 786436
  605.4 76.7 %copy-start.1 = (bf16[1024,128]{1,0:T(8,128)(2,1)}, bf16[1024,128]{1,0:T(8,128)(2,1)S(1)}, u32[]{:S(2)}) copy-start(bf16[1024,128]{1,0:T(8,128)(2,1)S(1)} %scatter_fusion.1) | copy-start | bytes 786436
Sparse Core Ops, SparseCore 0:
  211.9 110.7 all-reduce.2
  602.8 77.8 reduce-scatter.1
where the time goes:
time: 690 us; the launch traced here: 689 us
  blocking collectives  311 us (45%)
  waiting for transfers between devices  292 us (42%)
  local copies, waits for them, and re-layouts  39.5 us (6%)
  between operations  17.8 us (3%)
  other arithmetic  12.3 us (2%)
  matrix products  12.3 us (2%)
    all_to_all x1, blocking collectives, body(): lax.all_to_all(send_rows, 'wide', split_axis=0, concat_axis=0, tiled=True)  127 us
    psum x1, waiting for transfers between devices, body(): summed = lax.psum(partial_value, 'narrow')  109 us
    all_to_all x1, waiting for transfers between devices, body(): lax.all_to_all(produced, 'wide', split_axis=0, concat_axis=0, tiled=True)  108 us
    reduce_scatter x1, waiting for transfers between devices, body(): lax.psum_scatter(partial_moe, 'narrow', scatter_dimension=1, tiled=True)  75.3 us
    all_gather x1, blocking collectives, body(): lax.all_gather(prefix_values, 'wide', axis=0, tiled=True)  39 us
    all_gather x1, blocking collectives, body(): lax.all_gather(query_weight, 'wide', axis=0, tiled=True)  30 us
    all_gather x1, blocking collectives, body(): lax.all_gather(value_weight, 'wide', axis=0, tiled=True)  29.9 us
    all_gather x1, blocking collectives, body(): lax.all_gather(output_weight, 'wide', axis=0, tiled=True)  28.5 us
  transfers between devices with their start and end apart: 3, of which 3 were waited for; matrix products, arithmetic and copies ran while one was open for 1% of the time, Pallas kernels for 0%

commit v1 on v0

v1 whole, which is shorter than its diff:
```python
import math

import jax
import jax.numpy as jnp
from jax import lax
from jax.experimental import pallas as pl
from jax.experimental.pallas import tpu as pltpu
from jax.sharding import PartitionSpec as P

HD = 128
E = 64
SINK = 4
WIN = 512
CAP = 9
NX = 4
NY = 4
MESH = pl.DeviceIdType.MESH
F32 = jnp.float32
BF16 = jnp.bfloat16

norm_eps = 1e-06


def rms_scale(rows, row_gain):
    widened = rows.astype(F32)
    power_mean = jnp.mean(widened * widened, axis=-1, keepdims=True)
    return (widened * lax.rsqrt(power_mean + norm_eps) * row_gain).astype(BF16)


def tree_links(parents):
    tree_size = parents.shape[-1]
    node_ids = jnp.arange(tree_size, dtype=jnp.int32)
    linked = (node_ids[:, None] == node_ids[None, :]) | (parents[0][:, None] == node_ids)
    for _ in range(6):
        m = linked.astype(BF16)
        linked = jnp.dot(m, m, preferred_element_type=F32) > 0.5
    depths = jnp.sum(linked.astype(jnp.int32), axis=-1) - 1
    return linked, depths


def rcopy(src, dst, ssem, rsem, dev):
    return pltpu.make_async_remote_copy(
        src_ref=src, dst_ref=dst, send_sem=ssem, recv_sem=rsem, device_id=dev, device_id_type=MESH
    )


def wide_barrier(w, n, nw):
    barrier = pltpu.get_barrier_semaphore()

    def sig(d, _):
        pl.semaphore_signal(barrier, inc=1, device_id=(lax.rem(w + d, nw), n), device_id_type=MESH)
        return 0

    lax.fori_loop(1, nw, sig, 0)
    pl.semaphore_wait(barrier, nw - 1)


def narrow_barrier(w, n, nn):
    barrier = pltpu.get_barrier_semaphore()

    def sig(d, _):
        pl.semaphore_signal(barrier, inc=1, device_id=(w, lax.rem(n + d, nn)), device_id_type=MESH)
        return 0

    lax.fori_loop(1, nn, sig, 0)
    pl.semaphore_wait(barrier, nn - 1)


def gather_kernel(nw, q, k, v, o, ps, gq, gk, gv, go, pr, rs, rr, bs, br, fs, fr, pss, psr, ls):
    nz = nw // 2
    hops_r = nz // 2
    hops_l = nz - 1 - hops_r
    w = lax.axis_index("wide")
    n = lax.axis_index("narrow")
    z = w // 2
    c = lax.rem(w, 2)
    sib = (w + 1 - 2 * c, n)
    right = (lax.rem(z + 1, nz) * 2 + c, n)
    left = (lax.rem(z + nz - 1, nz) * 2 + c, n)
    ins = (q, k, v, o)
    outs = (gq, gk, gv, go)
    wide_barrier(w, n, nw)

    def blk(off):
        return lax.rem(z + off + nz, nz) * 2 + c

    local = []
    for i in range(4):
        cp = pltpu.make_async_copy(ins[i], outs[i].at[w], ls.at[i])
        cp.start()
        local.append(cp)
        rcopy(ins[i], outs[i].at[w], rs.at[i, 0], rr.at[i, 0], right).start()
        rcopy(ins[i], outs[i].at[w], bs.at[i, 0], br.at[i, 0], left).start()
        rcopy(ins[i], outs[i].at[w], fs.at[i, 0], fr.at[i, 0], sib).start()
    cp = pltpu.make_async_copy(ps.at[w], pr.at[w], ls.at[4])
    cp.start()
    local.append(cp)

    def psend(d, _):
        t = lax.rem(w + d, nw)
        rcopy(ps.at[t], pr.at[w], pss.at[d], psr.at[w], (t, n)).start()
        return 0

    lax.fori_loop(1, nw, psend, 0)

    def pass_right(i, s, on):
        ref = outs[i].at[blk(-s)]
        rcopy(ref, ref, rs.at[i, s - 1], rr.at[i, s - 1], right).wait_recv()
        if on:
            rcopy(ref, ref, rs.at[i, s], rr.at[i, s], right).start()
        rcopy(ref, ref, fs.at[i, s], fr.at[i, s], sib).start()

    def pass_left(i, s, on):
        ref = outs[i].at[blk(s)]
        rcopy(ref, ref, bs.at[i, s - 1], br.at[i, s - 1], left).wait_recv()
        if on:
            rcopy(ref, ref, bs.at[i, s], br.at[i, s], left).start()
        rcopy(ref, ref, fs.at[i, hops_r + s], fr.at[i, hops_r + s], sib).start()

    def step(s, _):
        for i in range(4):
            pass_right(i, s, True)
            pass_left(i, s, True)
        return 0

    lax.fori_loop(1, hops_l, step, 0)
    for i in range(4):
        pass_right(i, hops_l, True)
        pass_left(i, hops_l, False)
    for i in range(4):
        pass_right(i, hops_r, False)
    for cp in local:
        cp.wait()

    def done_sib(s, _):
        for i in range(4):
            ref = outs[i].at[0]
            d = rcopy(ref, ref, fs.at[i, s], fr.at[i, s], sib)
            d.wait_recv()
            d.wait_send()
        return 0

    lax.fori_loop(0, nz, done_sib, 0)

    def done_r(s, _):
        for i in range(4):
            ref = outs[i].at[0]
            rcopy(ref, ref, rs.at[i, s], rr.at[i, s], right).wait_send()
        return 0

    lax.fori_loop(0, hops_r, done_r, 0)

    def done_l(s, _):
        for i in range(4):
            ref = outs[i].at[0]
            rcopy(ref, ref, bs.at[i, s], br.at[i, s], left).wait_send()
        return 0

    lax.fori_loop(0, hops_l, done_l, 0)

    def pdone(d, _):
        t = lax.rem(w + d, nw)
        cp = rcopy(ps.at[t], pr.at[t], pss.at[d], psr.at[t], (t, n))
        cp.wait_recv()
        cp.wait_send()
        return 0

    lax.fori_loop(1, nw, pdone, 0)


def gather_call(nw, q, k, v, o, ps):
    nz = nw // 2
    vm = pl.BlockSpec(memory_space=pltpu.VMEM)
    hop = nz // 2
    dma = pltpu.SemaphoreType.DMA
    full = jax.ShapeDtypeStruct((nw,) + q.shape, BF16)
    return pl.pallas_call(
        lambda *refs: gather_kernel(nw, *refs),
        out_shape=(full,) * 4 + (jax.ShapeDtypeStruct(ps.shape, BF16),),
        in_specs=[vm] * 5,
        out_specs=(vm,) * 5,
        scratch_shapes=[
            dma((4, hop)), dma((4, hop)), dma((4, hop)), dma((4, hop)),
            dma((4, nz)), dma((4, nz)), dma((nw,)), dma((nw,)), dma((5,)),
        ],
        compiler_params=pltpu.CompilerParams(collective_id=0, has_side_effects=True),
        name="weights_gather",
    )(q, k, v, o, ps)


def proj_kernel(nn, part, hid, out, rbuf, mine, s1, r1, s2, r2, ls):
    w = lax.axis_index("wide")
    n = lax.axis_index("narrow")
    narrow_barrier(w, n, nn)

    def send1(d, _):
        t = lax.rem(n + d, nn)
        rcopy(part.at[t], rbuf.at[n], s1.at[d], r1.at[n], (w, t)).start()
        return 0

    lax.fori_loop(1, nn, send1, 0)

    def add(d, acc):
        t = lax.rem(n + d, nn)
        cp = rcopy(part.at[t], rbuf.at[t], s1.at[d], r1.at[t], (w, t))
        cp.wait_recv()
        cp.wait_send()
        return acc + rbuf[t].astype(F32)

    total = lax.fori_loop(1, nn, add, part[n].astype(F32))
    mine[...] = (hid[...].astype(F32) + total).astype(BF16)

    def send2(d, _):
        t = lax.rem(n + d, nn)
        rcopy(mine, out.at[n], s2.at[d], r2.at[n], (w, t)).start()
        return 0

    lax.fori_loop(1, nn, send2, 0)
    cp = pltpu.make_async_copy(mine, out.at[n], ls)
    cp.start()
    cp.wait()

    def done(d, _):
        t = lax.rem(n + d, nn)
        cp = rcopy(mine, out.at[t], s2.at[d], r2.at[t], (w, t))
        cp.wait_recv()
        cp.wait_send()
        return 0

    lax.fori_loop(1, nn, done, 0)


def proj_call(nn, part, hid):
    vm = pl.BlockSpec(memory_space=pltpu.VMEM)
    dma = pltpu.SemaphoreType.DMA
    return pl.pallas_call(
        lambda *refs: proj_kernel(nn, *refs),
        out_shape=jax.ShapeDtypeStruct(part.shape, BF16),
        in_specs=[vm] * 2,
        out_specs=vm,
        scratch_shapes=[
            pltpu.VMEM(part.shape, BF16), pltpu.VMEM(hid.shape, BF16),
            dma((nn,)), dma((nn,)), dma((nn,)), dma((nn,)), dma,
        ],
        compiler_params=pltpu.CompilerParams(collective_id=1, has_side_effects=True),
        name="proj_sum",
    )(part, hid)


def swap_kernel(nw, src, dst, ss, rr, ls):
    w = lax.axis_index("wide")
    n = lax.axis_index("narrow")
    wide_barrier(w, n, nw)

    def send(d, _):
        t = lax.rem(w + d, nw)
        rcopy(src.at[t], dst.at[w], ss.at[d], rr.at[w], (t, n)).start()
        return 0

    lax.fori_loop(1, nw, send, 0)
    cp = pltpu.make_async_copy(src.at[w], dst.at[w], ls)
    cp.start()
    cp.wait()

    def done(d, _):
        t = lax.rem(w + d, nw)
        cp = rcopy(src.at[t], dst.at[t], ss.at[d], rr.at[t], (t, n))
        cp.wait_recv()
        cp.wait_send()
        return 0

    lax.fori_loop(1, nw, done, 0)


def swap_call(nw, src, cid, name):
    vm = pl.BlockSpec(memory_space=pltpu.VMEM)
    dma = pltpu.SemaphoreType.DMA
    return pl.pallas_call(
        lambda *refs: swap_kernel(nw, *refs),
        out_shape=jax.ShapeDtypeStruct(src.shape, BF16),
        in_specs=[vm],
        out_specs=vm,
        scratch_shapes=[dma((nw,)), dma((nw,)), dma],
        compiler_params=pltpu.CompilerParams(collective_id=cid, has_side_effects=True),
        name=name,
    )(src)


CHUNKS = 4
LOW = 80


def plane_ids():
    w = lax.axis_index("wide")
    n = lax.axis_index("narrow")
    y = n // NX
    x = lax.rem(n, NX)
    return w, n, y, x


def spread_kernel(rows, src, out, ss, rr, ls):
    w, n, y, x = plane_ids()
    size = rows // CHUNKS
    barrier = pltpu.get_barrier_semaphore()

    def dev(axis, off):
        if axis == 0:
            return (w, y * NX + lax.rem(x + off + NX, NX))
        return (w, lax.rem(y + off + NY, NY) * NX + x)

    for axis in (0, 1):
        for off in (1, -1):
            pl.semaphore_signal(barrier, inc=1, device_id=dev(axis, off), device_id_type=MESH)
    pl.semaphore_wait(barrier, 4)

    def ref_at(axis, b, o, lo, ln):
        if axis == 0:
            return out.at[o, b, pl.ds(lo, ln), :]
        return out.at[b, o, pl.ds(lo, ln), :]

    def pos(axis, off):
        if axis == 0:
            return lax.rem(x + off + NX, NX)
        return lax.rem(y + off + NY, NY)

    own = []
    for j in range(CHUNKS):
        lo = j * size
        axis = j % 2
        cp = pltpu.make_async_copy(
            src.at[pl.ds(lo, size), :], out.at[y, x, pl.ds(lo, size), :], ls.at[j]
        )
        cp.start()
        own.append(cp)
        dst = out.at[y, x, pl.ds(lo, size), :]
        a = src.at[pl.ds(lo, size), :]
        rcopy(a, dst, ss.at[j, 0], rr.at[j, 0], dev(axis, 1)).start()
        rcopy(a, dst, ss.at[j, 1], rr.at[j, 1], dev(axis, -1)).start()
        rcopy(a, dst, ss.at[j, 4], rr.at[j, 4], dev(1 - axis, 1)).start()
        rcopy(a, dst, ss.at[j, 5], rr.at[j, 5], dev(1 - axis, -1)).start()

    def desc(j, slot, b, o, lo, ln, to):
        r = ref_at(j % 2, b, o, lo, ln)
        return rcopy(r, r, ss.at[j, slot], rr.at[j, slot], to)

    pending = []

    def go(d):
        d.start()
        pending.append(d)

    for j in range(CHUNKS):
        lo = j * size
        axis = j % 2
        me_o = pos(1 - axis, 0)
        bm, bp, b2 = pos(axis, -1), pos(axis, 1), pos(axis, 2)
        desc(j, 0, bm, me_o, lo, size, dev(axis, 1)).wait_recv()
        desc(j, 2, bm, me_o, lo, LOW, dev(axis, 1)).start()
        desc(j, 8, bm, me_o, lo, size, dev(1 - axis, 1)).start()
        desc(j, 9, bm, me_o, lo, size, dev(1 - axis, -1)).start()
        desc(j, 1, bp, me_o, lo, size, dev(axis, -1)).wait_recv()
        desc(j, 3, bp, me_o, lo + LOW, size - LOW, dev(axis, -1)).start()
        desc(j, 12, bp, me_o, lo, size, dev(1 - axis, 1)).start()
        desc(j, 13, bp, me_o, lo, size, dev(1 - axis, -1)).start()
    for j in range(CHUNKS):
        lo = j * size
        axis = j % 2
        me_o = pos(1 - axis, 0)
        b0, bm, bp, b2 = pos(axis, 0), pos(axis, -1), pos(axis, 1), pos(axis, 2)
        om, op, o2 = pos(1 - axis, -1), pos(1 - axis, 1), pos(1 - axis, 2)
        desc(j, 4, b0, om, lo, size, dev(1 - axis, 1)).wait_recv()
        desc(j, 6, b0, om, lo, LOW, dev(1 - axis, 1)).start()
        desc(j, 5, b0, op, lo, size, dev(1 - axis, -1)).wait_recv()
        desc(j, 7, b0, op, lo + LOW, size - LOW, dev(1 - axis, -1)).start()
        desc(j, 2, b2, me_o, lo, LOW, dev(axis, 1)).wait_recv()
        desc(j, 3, b2, me_o, lo + LOW, size - LOW, dev(axis, -1)).wait_recv()
        desc(j, 16, b2, me_o, lo, size, dev(1 - axis, 1)).start()
        desc(j, 17, b2, me_o, lo, size, dev(1 - axis, -1)).start()
        for base, b in ((8, bm), (12, bp)):
            desc(j, base, b, om, lo, size, dev(1 - axis, 1)).wait_recv()
            desc(j, base + 2, b, om, lo, LOW, dev(1 - axis, 1)).start()
            desc(j, base + 1, b, op, lo, size, dev(1 - axis, -1)).wait_recv()
            desc(j, base + 3, b, op, lo + LOW, size - LOW, dev(1 - axis, -1)).start()
    for j in range(CHUNKS):
        lo = j * size
        axis = j % 2
        b2 = pos(axis, 2)
        om, op, o2 = pos(1 - axis, -1), pos(1 - axis, 1), pos(1 - axis, 2)
        desc(j, 16, b2, om, lo, size, dev(1 - axis, 1)).wait_recv()
        desc(j, 18, b2, om, lo, LOW, dev(1 - axis, 1)).start()
        desc(j, 17, b2, op, lo, size, dev(1 - axis, -1)).wait_recv()
        desc(j, 19, b2, op, lo + LOW, size - LOW, dev(1 - axis, -1)).start()
    for j in range(CHUNKS):
        lo = j * size
        axis = j % 2
        o2 = pos(1 - axis, 2)
        for base, off in ((4, 0), (8, -1), (12, 1), (16, 2)):
            b = pos(axis, off)
            desc(j, base + 2, b, o2, lo, LOW, dev(1 - axis, 1)).wait_recv()
            desc(j, base + 3, b, o2, lo + LOW, size - LOW, dev(1 - axis, -1)).wait_recv()
    for cp in own:
        cp.wait()
    for j in range(CHUNKS):
        for slot in range(20):
            if slot < 2 or slot % 4 < 2:
                lo, ln = 0, size
            elif slot % 4 == 2:
                lo, ln = 0, LOW
            else:
                lo, ln = LOW, size - LOW
            desc(j, slot, 0, 0, lo, ln, dev(0, 1)).wait_send()


def spread_call(src):
    rows = src.shape[0]
    vm = pl.BlockSpec(memory_space=pltpu.VMEM)
    dma = pltpu.SemaphoreType.DMA
    return pl.pallas_call(
        lambda *refs: spread_kernel(rows, *refs),
        out_shape=jax.ShapeDtypeStruct((NY, NX) + src.shape, BF16),
        in_specs=[vm],
        out_specs=vm,
        scratch_shapes=[dma((CHUNKS, 20)), dma((CHUNKS, 20)), dma((CHUNKS,))],
        compiler_params=pltpu.CompilerParams(collective_id=3, has_side_effects=True),
        name="plane_spread",
    )(src)


def fold_kernel(rows, src, out, r1, f1, t1, m2, r2, f2, t2, ss, rr, ls):
    w, n, y, x = plane_ids()
    size = rows // CHUNKS
    barrier = pltpu.get_barrier_semaphore()

    def dev(axis, off):
        if axis == 0:
            return (w, y * NX + lax.rem(x + off + NX, NX))
        return (w, lax.rem(y + off + NY, NY) * NX + x)

    for axis in (0, 1):
        for off in (1, -1):
            pl.semaphore_signal(barrier, inc=1, device_id=dev(axis, off), device_id_type=MESH)
    pl.semaphore_wait(barrier, 4)

    def pos(axis, off):
        if axis == 0:
            return lax.rem(x + off + NX, NX)
        return lax.rem(y + off + NY, NY)

    def src_at(axis, b, lo, ln):
        if axis == 0:
            return src.at[:, b, pl.ds(lo, ln), :]
        return src.at[b, :, pl.ds(lo, ln), :]

    def val(axis, b, lo, ln):
        if axis == 0:
            return src[:, b, pl.ds(lo, ln), :].astype(F32)
        return src[b, :, pl.ds(lo, ln), :].astype(F32)

    for j in range(CHUNKS):
        axis, lo = j % 2, j * size
        b2 = pos(axis, 2)
        rcopy(src_at(axis, b2, lo, LOW), f1.at[j, :, pl.ds(0, LOW), :],
              ss.at[j, 0], rr.at[j, 0], dev(axis, 1)).start()
        rcopy(src_at(axis, b2, lo + LOW, size - LOW), f1.at[j, :, pl.ds(LOW, size - LOW), :],
              ss.at[j, 1], rr.at[j, 1], dev(axis, -1)).start()

    def d1(j, slot, lo, ln, to):
        r = f1.at[j, :, pl.ds(lo, ln), :]
        return rcopy(r, r, ss.at[j, slot], rr.at[j, slot], to)

    for j in range(CHUNKS):
        axis, lo = j % 2, j * size
        bp, bm = pos(axis, 1), pos(axis, -1)
        d1(j, 0, 0, LOW, dev(axis, 1)).wait_recv()
        t1[j, 0, :, pl.ds(0, LOW), :] = (
            val(axis, bp, lo, LOW) + f1[j, :, pl.ds(0, LOW), :].astype(F32)
        ).astype(BF16)
        t1[j, 0, :, pl.ds(LOW, size - LOW), :] = val(axis, bp, lo + LOW, size - LOW).astype(BF16)
        rcopy(t1.at[j, 0], r1.at[j, 0], ss.at[j, 2], rr.at[j, 2], dev(axis, 1)).start()
        d1(j, 1, LOW, size - LOW, dev(axis, -1)).wait_recv()
        t1[j, 1, :, pl.ds(LOW, size - LOW), :] = (
            val(axis, bm, lo + LOW, size - LOW) + f1[j, :, pl.ds(LOW, size - LOW), :].astype(F32)
        ).astype(BF16)
        t1[j, 1, :, pl.ds(0, LOW), :] = val(axis, bm, lo, LOW).astype(BF16)
        rcopy(t1.at[j, 1], r1.at[j, 1], ss.at[j, 3], rr.at[j, 3], dev(axis, -1)).start()

    for j in range(CHUNKS):
        axis, lo = j % 2, j * size
        for k in range(2):
            rcopy(t1.at[j, k], r1.at[j, k], ss.at[j, 2 + k], rr.at[j, 2 + k], dev(axis, 1)).wait_recv()
        m2[j] = (
            val(axis, pos(axis, 0), lo, size) + r1[j, 0].astype(F32) + r1[j, 1].astype(F32)
        ).astype(BF16)
        b2 = pos(1 - axis, 2)
        rcopy(m2.at[j, b2, pl.ds(0, LOW), :], f2.at[j, pl.ds(0, LOW), :],
              ss.at[j, 4], rr.at[j, 4], dev(1 - axis, 1)).start()
        rcopy(m2.at[j, b2, pl.ds(LOW, size - LOW), :], f2.at[j, pl.ds(LOW, size - LOW), :],
              ss.at[j, 5], rr.at[j, 5], dev(1 - axis, -1)).start()

    def d2(j, slot, lo, ln, to):
        r = f2.at[j, pl.ds(lo, ln), :]
        return rcopy(r, r, ss.at[j, slot], rr.at[j, slot], to)

    for j in range(CHUNKS):
        axis = j % 2
        bp, bm = pos(1 - axis, 1), pos(1 - axis, -1)
        d2(j, 4, 0, LOW, dev(1 - axis, 1)).wait_recv()
        t2[j, 0, pl.ds(0, LOW), :] = (
            m2[j, bp, pl.ds(0, LOW), :].astype(F32) + f2[j, pl.ds(0, LOW), :].astype(F32)
        ).astype(BF16)
        t2[j, 0, pl.ds(LOW, size - LOW), :] = m2[j, bp, pl.ds(LOW, size - LOW), :]
        rcopy(t2.at[j, 0], r2.at[j, 0], ss.at[j, 6], rr.at[j, 6], dev(1 - axis, 1)).start()
        d2(j, 5, LOW, size - LOW, dev(1 - axis, -1)).wait_recv()
        t2[j, 1, pl.ds(LOW, size - LOW), :] = (
            m2[j, bm, pl.ds(LOW, size - LOW), :].astype(F32) + f2[j, pl.ds(LOW, size - LOW), :].astype(F32)
        ).astype(BF16)
        t2[j, 1, pl.ds(0, LOW), :] = m2[j, bm, pl.ds(0, LOW), :]
        rcopy(t2.at[j, 1], r2.at[j, 1], ss.at[j, 7], rr.at[j, 7], dev(1 - axis, -1)).start()
    for j in range(CHUNKS):
        axis = j % 2
        for k in range(2):
            rcopy(t2.at[j, k], r2.at[j, k], ss.at[j, 6 + k], rr.at[j, 6 + k], dev(0, 1)).wait_recv()
        out[pl.ds(j * size, size), :] = (
            m2[j, pos(1 - axis, 0)].astype(F32) + r2[j, 0].astype(F32) + r2[j, 1].astype(F32)
        ).astype(BF16)
    for j in range(CHUNKS):
        d1(j, 0, 0, LOW, dev(0, 1)).wait_send()
        d1(j, 1, LOW, size - LOW, dev(0, 1)).wait_send()
        d2(j, 4, 0, LOW, dev(0, 1)).wait_send()
        d2(j, 5, LOW, size - LOW, dev(0, 1)).wait_send()
        for k in range(2):
            rcopy(t1.at[j, k], r1.at[j, k], ss.at[j, 2 + k], rr.at[j, 2 + k], dev(0, 1)).wait_send()
            rcopy(t2.at[j, k], r2.at[j, k], ss.at[j, 6 + k], rr.at[j, 6 + k], dev(0, 1)).wait_send()


def fold_call(src):
    rows = src.shape[2]
    size = rows // CHUNKS
    vm = pl.BlockSpec(memory_space=pltpu.VMEM)
    dma = pltpu.SemaphoreType.DMA
    return pl.pallas_call(
        lambda *refs: fold_kernel(rows, *refs),
        out_shape=jax.ShapeDtypeStruct((rows, 128), BF16),
        in_specs=[vm],
        out_specs=vm,
        scratch_shapes=[
            pltpu.VMEM((CHUNKS, 2, 4, size, 128), BF16),
            pltpu.VMEM((CHUNKS, 4, size, 128), BF16),
            pltpu.VMEM((CHUNKS, 2, 4, size, 128), BF16),
            pltpu.VMEM((CHUNKS, 4, size, 128), BF16),
            pltpu.VMEM((CHUNKS, 2, size, 128), BF16),
            pltpu.VMEM((CHUNKS, size, 128), BF16),
            pltpu.VMEM((CHUNKS, 2, size, 128), BF16),
            dma((CHUNKS, 8)), dma((CHUNKS, 8)), dma,
        ],
        compiler_params=pltpu.CompilerParams(collective_id=4, has_side_effects=True),
        name="plane_fold",
    )(src)


def body(
    hidden,
    attn_gain,
    expert_gain,
    query_weight,
    key_weight,
    value_weight,
    output_weight,
    router_weight,
    gate_weight,
    up_weight,
    down_weight,
    prefix_keys,
    prefix_values,
    cache_keys,
    cache_values,
    parents,
    cache_lengths,
    group_ids,
    expert_ids,
    accepted,
):
    tok, width = hidden.shape
    cache_size = cache_keys.shape[1]
    nn = lax.axis_size("narrow")
    nw = lax.axis_size("wide")
    n = lax.axis_index("narrow")
    slice_width = width // nn
    top = expert_ids.shape[1]
    exp_local = gate_weight.shape[0]
    per_dev = exp_local * CAP
    slots_all = nw * per_dev
    scale_factor = 1.0 / math.sqrt(HD)
    pre = jnp.concatenate([prefix_keys, prefix_values], axis=0)
    psend = jnp.transpose(jnp.take(pre, group_ids, axis=1), (1, 0, 2))
    gq, gk, gv, go, pr = gather_call(nw, query_weight, key_weight, value_weight, output_weight, psend)
    pp = prefix_keys.shape[0]
    group_keys = pr[:, :pp].reshape(nw * pp, HD)
    group_values = pr[:, pp:].reshape(nw * pp, HD)
    normed = rms_scale(hidden, attn_gain)

    def project(g):
        return jnp.dot(normed, g.reshape(width, HD), preferred_element_type=F32).astype(BF16)

    queries, keys_new, values_new = project(gq), project(gk), project(gv)
    length = cache_lengths[0]
    slot_ids = jnp.arange(cache_size, dtype=jnp.int32)
    cache_mask = (slot_ids < length) & ((slot_ids < SINK) | (slot_ids >= length - WIN))
    ancestry, depths = tree_links(parents)
    own_keys, own_values = cache_keys[0], cache_values[0]

    def score(k):
        return (
            lax.dot_general(queries, k, (((1,), (1,)), ((), ())), preferred_element_type=F32)
            * scale_factor
        )

    ps, cs, ts = score(group_keys), score(own_keys), score(keys_new)
    cs = jnp.where(cache_mask[None, :], cs, -jnp.inf)
    ts = jnp.where(ancestry, ts, -jnp.inf)
    row_top = jnp.maximum(
        jnp.max(ps, axis=-1), jnp.maximum(jnp.max(cs, axis=-1), jnp.max(ts, axis=-1))
    )[:, None]
    pw, cw, tw = jnp.exp(ps - row_top), jnp.exp(cs - row_top), jnp.exp(ts - row_top)
    row_total = jnp.sum(pw, axis=-1) + jnp.sum(cw, axis=-1) + jnp.sum(tw, axis=-1)

    def weigh(wt, v):
        return jnp.dot(wt.astype(BF16), v, preferred_element_type=F32)

    weighted = weigh(pw, group_values) + weigh(cw, own_values) + weigh(tw, values_new)
    attended = (weighted / row_total[:, None]).astype(BF16)
    part = lax.dot_general(
        go.reshape(nn, slice_width, HD), attended, (((2,), (1,)), ((), ())), preferred_element_type=F32
    )
    part = jnp.transpose(part, (0, 2, 1)).astype(BF16)
    hid_slice = lax.dynamic_slice_in_dim(hidden, n * slice_width, slice_width, 1)
    mixed_all = proj_call(nn, part, hid_slice)
    mixed = jnp.transpose(mixed_all, (1, 0, 2)).reshape(tok, width)
    mixed_part = lax.dynamic_index_in_dim(mixed_all, n, 0, keepdims=False)
    normed_moe = rms_scale(mixed, expert_gain)
    logits = jnp.dot(normed_moe, router_weight, preferred_element_type=F32)
    expert_range = jnp.arange(E, dtype=jnp.int32)
    matches = expert_ids[:, :, None] == expert_range
    chosen = jnp.sum(jnp.where(matches, logits[:, None, :], 0.0), axis=-1)
    shares = jax.nn.softmax(chosen, axis=-1)
    named = jnp.any(matches, axis=1)
    tok_ids = jnp.arange(tok, dtype=jnp.int32)
    before = (tok_ids[:, None] > tok_ids[None, :]).astype(BF16)
    earlier = jnp.dot(before, named.astype(BF16), preferred_element_type=F32)
    ranks = jnp.sum(jnp.where(matches, earlier[:, None, :], 0.0), axis=-1).astype(jnp.int32)
    targets = expert_ids * CAP + ranks
    slot_range = jnp.arange(slots_all, dtype=jnp.int32)
    hit = targets[:, :, None] == slot_range
    place = jnp.any(hit, axis=1).astype(BF16)
    normed_slice = lax.dynamic_slice_in_dim(normed_moe, n * slice_width, slice_width, 1)
    send = lax.dot_general(
        place, normed_slice, (((0,), (0,)), ((), ())), preferred_element_type=F32
    ).astype(BF16)
    routed = swap_call(nw, send.reshape(nw, per_dev // 2, 2, slice_width), 2, "dispatch")
    rows = spread_call(routed.reshape(slots_all, slice_width))
    rows = rows.reshape(nn, slots_all, slice_width)
    fw = gate_weight.shape[2]
    both = jnp.concatenate([gate_weight[0], gate_weight[1], up_weight[0], up_weight[1]], axis=1)
    hidden_units = jnp.einsum(
        "nrd,ndf->rf", rows, both.reshape(nn, slice_width, 4 * fw), preferred_element_type=F32
    )
    act = jax.nn.silu(hidden_units[:, : 2 * fw]) * hidden_units[:, 2 * fw :]
    second = (slot_range % per_dev) >= CAP
    cols = jnp.arange(2 * fw, dtype=jnp.int32) >= fw
    act = jnp.where(second[:, None] == cols[None, :], act, 0.0).astype(BF16)
    down = down_weight.reshape(2 * fw, nn, slice_width)
    pieces = jnp.einsum("rf,fnd->nrd", act, down, preferred_element_type=F32).astype(BF16)
    folded = fold_call(pieces.reshape(NY, NX, slots_all, slice_width))
    back = swap_call(nw, folded.reshape(nw, per_dev // 2, 2, slice_width), 5, "return")
    back = back.reshape(slots_all, slice_width)
    mix = jnp.sum(jnp.where(hit, shares[:, :, None], 0.0), axis=1)
    moe_part = jnp.dot(mix, back.astype(F32), precision=lax.Precision.HIGHEST)
    layer_out = (mixed_part.astype(F32) + moe_part).astype(BF16)
    on_path = lax.dynamic_index_in_dim(ancestry, accepted[0], 0, keepdims=False)
    slots = jnp.where(on_path, length + depths, cache_size)
    put = slot_ids[:, None] == slots[None, :]
    written = jnp.any(put, axis=1)[:, None]
    put = put.astype(BF16)

    def compact(cache, fresh):
        moved = jnp.dot(put, fresh, preferred_element_type=F32).astype(BF16)
        return jnp.where(written, moved, cache)[None]

    new_keys = compact(own_keys, keys_new)
    new_values = compact(own_values, values_new)
    return (layer_out, new_keys, new_values)


def solution(mesh):
    in_specs = (
        P("wide", None),
        P(),
        P(),
        P("wide", "narrow"),
        P("wide", "narrow"),
        P("wide", "narrow"),
        P("wide", "narrow"),
        P(),
        P("wide", None, "narrow"),
        P("wide", None, "narrow"),
        P("wide", "narrow", None),
        P("wide", None, "narrow"),
        P("wide", None, "narrow"),
        P("wide", None, "narrow"),
        P("wide", None, "narrow"),
        P("wide", None),
        P("wide"),
        P(),
        P("wide", None),
        P("wide"),
    )
    out_specs = (P("wide", "narrow"), P("wide", None, "narrow"), P("wide", None, "narrow"))
    return jax.shard_map(body, mesh=mesh, in_specs=in_specs, out_specs=out_specs, check_vma=False)
```

time: 690 us -> 197 us (0.29)
  blocking collectives: 311 us -> 0 us
  waiting for transfers between devices: 292 us -> 0 us
  Pallas kernels: 0 us -> 158 us
  local copies, waits for them, and re-layouts: 39.5 us -> 11.9 us
  between operations: 17.8 us -> 2.37 us
    all_gather x6 -> x0, blocking collectives: 184 us -> none  [the longest x1 39 us: body(): lax.all_gather(prefix_values, 'wide', axis=0, tiled=True)]
    pallas_call x0 -> x6, Pallas kernels: none -> 158 us  [the longest x1 52.9 us: gather_call(): pl.pallas_call(lambda *refs: gather_kernel(nw, *refs), out_shape=(full,)...]
    all_to_all x1 -> x0, blocking collectives: 127 us -> none  [body(): lax.all_to_all(send_rows, 'wide', split_axis=0, concat_axis=0, tiled=True)]
    psum x1 -> x0, waiting for transfers between devices: 109 us -> none  [body(): summed = lax.psum(partial_value, 'narrow')]
    all_to_all x1 -> x0, waiting for transfers between devices: 108 us -> none  [body(): lax.all_to_all(produced, 'wide', split_axis=0, concat_axis=0, tiled=True)]
    reduce_scatter x1 -> x0, waiting for transfers between devices: 75.3 us -> none  [body(): lax.psum_scatter(partial_moe, 'narrow', scatter_dimension=1, tiled=True)]
    reshape x3 -> x0, local copies, waits for them, and re-layouts: 11 us -> none  [the longest x2 7.64 us: body(): send_rows = send_rows.reshape(wide_count, exp_local, CAP, model_width)]
    slice x1 -> x6, local copies, waits for them, and re-layouts: 0.23 us -> 8.62 us  [the longest x2 3.75 us: body(): up_weight[0]]
  transfers between devices with their start and end apart: 3 -> 0, of which waited for: 3 -> 0; matrix products, arithmetic and copies ran while one was open for 1% -> 0% of each run, Pallas kernels for 0% -> 0%
where the time goes in v1:
time: 197 us; the launch traced here: 196 us
  Pallas kernels  158 us (80%)
  matrix products  16.6 us (8%)
  local copies, waits for them, and re-layouts  11.9 us (6%)
  other arithmetic  7.81 us (4%)
  between operations  2.37 us (1%)
    pallas_call x1, Pallas kernels, gather_call(): pl.pallas_call(lambda *refs: gather_kernel(nw, *refs), out_shape=(full,)...  52.9 us
    pallas_call x2, Pallas kernels, swap_call(): pl.pallas_call(lambda *refs: swap_kernel(nw, *refs), out_shape=jax.ShapeD...  43.8 us
    pallas_call x1, Pallas kernels, fold_call(): pl.pallas_call(lambda *refs: fold_kernel(rows, *refs), out_shape=jax.Shap...  21.6 us
    pallas_call x1, Pallas kernels, spread_call(): pl.pallas_call(lambda *refs: spread_kernel(rows, *refs), out_shape=jax.Sh...  20.6 us
    pallas_call x1, Pallas kernels, proj_call(): pl.pallas_call(lambda *refs: proj_kernel(nn, *refs), out_shape=jax.ShapeD...  18.8 us

profile of v1, /device:TPU:1, one launch (start us, length us, event | category | flops | bytes accessed | tf_op | source)
XLA Modules:
  0.0 196.3 jit_solution(7272180124115475839)
XLA Ops:
  0.7 0.8 copy.56
  1.5 0.7 copy.57
  2.2 0.7 compare_select_fusion
  2.9 0.6 gather_fusion
  3.5 0.7 compare_and_fusion
  4.1 0.8 broadcast_select_fusion.refs_4_
  4.9 52.9 %weights_gather.1 = (bf16[32,64,128]{2,1,0:T(8,128)(2,1)}, bf16[32,64,128]{2,1,0:T(8,128)(2,1)}, bf16[32,64,128]{2,1,0:T(8,128)(2,1)}, bf16[32,64,128]{2,1,0:T(8,128)(2,1)}, bf16[32,16,128]{2,1,0:T(8,128)(2,1)}) custom-call(bf16[64,128]{1,0:T(8,128)(2,1)} %refs_0_.1, bf16[64,128]{1,0:T(8,128)(2,1)} %refs_1_.1, bf16[64,128]{1,0:T(8,128)(2,1)} %refs_2_.1, ...), custom_call_target="tpu_custom_call" | custom-call | tf_op jit(solution)/shard_map/weights_gather/pallas_call | solution.py:177
  57.8 1.2 fusion.19
  59.0 1.4 convolution_convert_fusion.7
  60.4 1.5 convolution_convert_fusion.6
  61.9 0.3 convolution_compare_fusion.4
  62.2 0.3 convolution_compare_fusion.2
  62.5 0.4 convert_reduce_fusion
  62.9 0.2 fusion.92
  63.1 0.3 fusion.90
  64.1 0.3 fusion.91
  64.4 0.2 fusion.56
  64.6 0.2 fusion.48
  64.8 0.2 fusion.33
  65.0 0.2 fusion.28
  65.3 0.2 convolution_add_fusion.2
  65.5 0.3 convolution_convert_fusion.5
  65.8 1.2 fusion.1.refs_0_
  67.0 0.6 constant_dynamic-slice_fusion.refs_1_
  67.6 18.8 %proj_sum.1 = bf16[16,64,128]{2,1,0:T(8,128)(2,1)} custom-call(bf16[16,64,128]{2,1,0:T(8,128)(2,1)} %fusion.1.refs_0_, bf16[64,128]{1,0:T(8,128)(2,1)} %constant_dynamic-slice_fusion.refs_1_), custom_call_target="tpu_custom_call" | custom-call | tf_op jit(solution)/shard_map/proj_sum/pallas_call | solution.py:236
  86.3 1.1 fusion.22
  87.5 1.1 fusion.24
  88.6 0.2 fusion.93
  88.9 0.2 fusion.32
  89.2 0.3 select_reduce_fusion.2
  89.7 0.5 fusion
  90.1 0.9 convolution_convert_fusion.4
  91.1 20.6 %dispatch.1 = bf16[32,9,2,128]{3,2,1,0:T(2,128)(2,1)} custom-call(bf16[32,9,2,128]{3,2,1,0:T(2,128)(2,1)} %bitcast.107), custom_call_target="tpu_custom_call" | custom-call | tf_op jit(solution)/shard_map/dispatch/pallas_call | solution.py:278
  111.7 20.6 %plane_spread.1 = bf16[4,4,576,128]{3,2,1,0:T(8,128)(2,1)} custom-call(bf16[576,128]{1,0:T(8,128)(2,1)} %bitcast.104), custom_call_target="tpu_custom_call" | custom-call | tf_op jit(solution)/shard_map/plane_spread/pallas_call | solution.py:418
  132.4 0.7 fusion.88
  133.1 2.1 %copy.66 = bf16[1,2048,64]{2,1,0:T(8,128)(2,1)} copy(bf16[1,2048,64]{1,2,0:T(8,128)(2,1)} %get-tuple-element.15) | data formatting | bytes 524288 | tf_op jit(solution)/shard_map/slice | solution.py:663
  135.2 1.0 copy.67
  136.2 1.8 fusion.89
  138.0 2.0 %copy.68 = bf16[1,2048,64]{2,1,0:T(8,128)(2,1)} copy(bf16[1,2048,64]{1,2,0:T(8,128)(2,1)} %get-tuple-element.17) | data formatting | bytes 524288 | tf_op jit(solution)/shard_map/slice | solution.py:663
  140.0 1.0 copy.69
  141.0 2.6 %convolution_bitcast_fusion = f32[576,256]{1,0:T(8,128)S(1)} fusion(bf16[16,576,128]{2,1,0:T(8,128)(2,1)S(1)} %bitcast.102, bf16[16,128,64]{2,1,0:T(8,128)(2,1)} %bitcast.111, bf16[16,128,64]{2,1,0:T(8,128)(2,1)} %bitcast.110, bf16[16,128,64]{2,1,0:T(8,128)(2,1)} %bitcast.109, bf16[16,128,64]{2,1,0:T(8,128)(2,1)} %bitcast.108), kind=kOutput, calls=%fused_computation.5 | convolution fusion | flops 608174080 | bytes 3997696 | tf_op jit(solution)/shard_map/nrd,ndf->rf/dot_general | solution.py:664
  143.7 2.2 %convolution_convert_fusion = bf16[576,16,128]{2,0,1:T(8,128)(2,1)} fusion(bf16[128,16,128]{2,1,0:T(8,128)(2,1)S(1)} %bitcast.103, f32[576,256]{1,0:T(8,128)S(1)} %convolution_bitcast_fusion, pred[128]{0:T(512)(128)(4,1)S(1)} %iota_compare_fusion.14, pred[576]{0:T(1024)(128)(4,1)S(1)} %fusion.69), kind=kOutput, calls=%fused_computation.1 | convolution fusion | flops 303759360 | bytes 3474112 | tf_op jit(solution)/shard_map/rf,fnd->nrd/dot_general | solution.py:672
  146.0 21.6 %plane_fold.1 = bf16[576,128]{1,0:T(8,128)(2,1)} custom-call(bf16[4,4,576,128]{3,2,1,0:T(8,128)(2,1)} %bitcast.101), custom_call_target="tpu_custom_call" | custom-call | tf_op jit(solution)/shard_map/plane_fold/pallas_call | solution.py:541
  167.6 23.1 %return.1 = bf16[32,9,2,128]{3,2,1,0:T(2,128)(2,1)} custom-call(bf16[32,9,2,128]{3,2,1,0:T(2,128)(2,1)} %bitcast.105), custom_call_target="tpu_custom_call" | custom-call | tf_op jit(solution)/shard_map/return/pallas_call | solution.py:278
  191.0 0.5 select_reduce_fusion
  191.5 1.7 fusion.10
  194.0 1.1 fusion.4
  195.1 1.1 fusion.6
  (50 shorter events, 1.0 us)
Async XLA Ops:
  0.6 87.9 %copy-start = (bf16[2048,64]{0,1:T(8,128)(2,1)S(1)}, bf16[2048,64]{0,1:T(8,128)(2,1)}, u32[]{:S(2)}) copy-start(bf16[2048,64]{0,1:T(8,128)(2,1)} %param.27) | copy-start | bytes 786436
  0.6 61.2 %copy-start.13 = (s32[1,64]{1,0:T(1,128)S(1)}, s32[1,64]{1,0:T(1,128)}, u32[]{:S(2)}) copy-start(s32[1,64]{1,0:T(1,128)} %param.35) | copy-start | bytes 772
  0.7 63.4 %copy-start.2 = (bf16[1,1024,128]{2,1,0:T(8,128)(2,1)S(1)}, bf16[1,1024,128]{2,1,0:T(8,128)(2,1)}, u32[]{:S(2)}) copy-start(bf16[1,1024,128]{2,1,0:T(8,128)(2,1)} %param.33) | copy-start | bytes 786436
  0.7 64.3 %copy-start.3 = (bf16[1,1024,128]{2,1,0:T(8,128)(2,1)S(1)}, bf16[1,1024,128]{2,1,0:T(8,128)(2,1)}, u32[]{:S(2)}) copy-start(bf16[1,1024,128]{2,1,0:T(8,128)(2,1)} %param.34) | copy-start | bytes 786436
  4.9 60.6 %copy-start.7 = (bf16[64,2048]{1,0:T(8,128)(2,1)S(1)}, bf16[64,2048]{1,0:T(8,128)(2,1)}, u32[]{:S(2)}) copy-start(bf16[64,2048]{1,0:T(8,128)(2,1)} %param.20) | copy-start | bytes 786436
  4.9 60.6 %copy-start.12 = (f32[2048]{0:T(1024)S(1)}, f32[2048]{0:T(1024)}, u32[]{:S(2)}) copy-start(f32[2048]{0:T(1024)} %param.21) | copy-start | bytes 24580
  57.8 5.3 %copy-start.8 = (bf16[32,16,128]{2,1,0:T(8,128)(2,1)S(1)}, bf16[32,16,128]{2,1,0:T(8,128)(2,1)}, u32[]{:S(2)}) copy-start(bf16[32,16,128]{2,1,0:T(8,128)(2,1)} %get-tuple-element.10) | copy-start | bytes 393220
  57.8 7.7 %copy-start.11 = (bf16[32,64,128]{2,1,0:T(8,128)(2,1)S(1)}, bf16[32,64,128]{2,1,0:T(8,128)(2,1)}, u32[]{:S(2)}) copy-start(bf16[32,64,128]{2,1,0:T(8,128)(2,1)} %get-tuple-element.12) | copy-start | bytes 1572868
  60.4 5.4 %copy-start.6 = (bf16[32,64,128]{2,1,0:T(8,128)(2,1)S(1)}, bf16[32,64,128]{2,1,0:T(8,128)(2,1)}, u32[]{:S(2)}) copy-start(bf16[32,64,128]{2,1,0:T(8,128)(2,1)} %get-tuple-element.8) | copy-start | bytes 1572868
  64.1 23.4 %copy-start.10 = (f32[2048]{0:T(1024)S(1)}, f32[2048]{0:T(1024)}, u32[]{:S(2)}) copy-start(f32[2048]{0:T(1024)} %param.22) | copy-start | bytes 24580
  65.0 23.8 %copy-start.9 = (s32[64,8]{0,1:T(8,128)S(1)}, s32[64,8]{0,1:T(8,128)}, u32[]{:S(2)}) copy-start(s32[64,8]{0,1:T(8,128)} %param.38) | copy-start | bytes 6148
  88.6 43.8 %copy-start.4 = (bf16[2,2048,64]{1,2,0:T(8,128)(2,1)S(1)}, bf16[2,2048,64]{1,2,0:T(8,128)(2,1)}, u32[]{:S(2)}) copy-start(bf16[2,2048,64]{1,2,0:T(8,128)(2,1)} %param.28) | copy-start | bytes 1572868
  133.1 7.9 %copy-start.1 = (bf16[4,4,576,128]{3,2,1,0:T(8,128)(2,1)S(1)}, bf16[4,4,576,128]{3,2,1,0:T(8,128)(2,1)}, u32[]{:S(2)}) copy-start(bf16[4,4,576,128]{3,2,1,0:T(8,128)(2,1)} %plane_spread.1) | copy-start | bytes 7077892
  141.0 2.6 %copy-start.5 = (bf16[2,64,2048]{2,1,0:T(8,128)(2,1)S(1)}, bf16[2,64,2048]{2,1,0:T(8,128)(2,1)}, u32[]{:S(2)}) copy-start(bf16[2,64,2048]{2,1,0:T(8,128)(2,1)} %param.30) | copy-start | bytes 1572868

commit v2 on v0

v2 whole, which is shorter than its diff:
```python
import math

import jax
import jax.numpy as jnp
from jax import lax
from jax.experimental import pallas as pl
from jax.experimental.pallas import tpu as pltpu
from jax.sharding import PartitionSpec as P

HD = 128
E = 64
SINK = 4
WIN = 512
CAP = 9
NX = 4
NY = 4
MESH = pl.DeviceIdType.MESH
F32 = jnp.float32
BF16 = jnp.bfloat16

norm_eps = 1e-06


def rms_scale(rows, row_gain):
    widened = rows.astype(F32)
    power_mean = jnp.mean(widened * widened, axis=-1, keepdims=True)
    return (widened * lax.rsqrt(power_mean + norm_eps) * row_gain).astype(BF16)


DIMS0 = (((0,), (0,)), ((), ()))
DIMS1 = (((1,), (1,)), ((), ()))
CHUNKS = 4
ORDER = (2, 1, 3, 0)
LOW = 80
NEG = -1e30


def rcopy(src, dst, ssem, rsem, dev):
    return pltpu.make_async_remote_copy(
        src_ref=src, dst_ref=dst, send_sem=ssem, recv_sem=rsem, device_id=dev, device_id_type=MESH
    )


def iota(shape, dim):
    return lax.broadcasted_iota(jnp.int32, shape, dim)


def mm(a, b, dims=(((1,), (0,)), ((), ()))):
    return lax.dot_general(a, b, dims, preferred_element_type=F32)


def layer_kernel(
    lens, acc_node, hidden, attn_gain, expert_gain, q_in, k_in, v_in, o_in, router, gate, up, down,
    pk, pv, cache_k, cache_v, parents, groups, ids,
    layer_out, new_k, new_v,
    normed, g, go, ps, pr, qs, ks, vs, cs, ts, anc, put, part, rbuf, mx, ssb, wgt, tgt, place, mix,
    dbuf, r, xs, src, r1, f1, t1, m2, r2, f2, t2, bbuf, bk,
    ls, rs, rr, fs, fr, os, orr, ofs, ofr, pss, psr, s1, r1s, s2, r2s, s3, r3s, ds, dr, ss, rrs, us, ur, es, er,
):
    nz, nn, nw = g.shape[0], part.shape[0], pr.shape[0]
    tok = hidden.shape[0]
    w = lax.axis_index("wide")
    n = lax.axis_index("narrow")
    z = w // 2
    c = lax.rem(w, 2)
    y = n // NX
    x = lax.rem(n, NX)
    sg = 1 - 2 * c
    sib_w = w + sg
    sib = (sib_w, n)

    def chip(off):
        return lax.rem(z + off + nz, nz)

    nxt = (chip(sg) * 2 + c, n)

    barrier = pltpu.get_barrier_semaphore()
    for t in (sib, (chip(1) * 2 + c, n), (chip(nz - 1) * 2 + c, n)):
        pl.semaphore_signal(barrier, inc=1, device_id=t, device_id_type=MESH)

    def greet(d, _):
        pl.semaphore_signal(barrier, inc=1, device_id=(w, lax.rem(n + d, nn)), device_id_type=MESH)
        return 0

    lax.fori_loop(1, nn, greet, 0)
    local = [
        pltpu.make_async_copy(a, b, ls.at[i])
        for i, (a, b) in enumerate(
            ((q_in, g.at[z, c, 0]), (k_in, g.at[z, c, 1]), (v_in, g.at[z, c, 2]), (o_in, go.at[z, c]))
        )
    ]
    for cp in local:
        cp.start()
    for cp in local:
        cp.wait()
    pl.semaphore_wait(barrier, nn + 2)

    def ring(s, sub):
        ref = g.at[chip(-sg * s), sub]
        return rcopy(ref, ref, rs.at[s, sub], rr.at[s, sub], nxt)

    def got(s, sub):
        ref = g.at[chip(-sg * (s + 1)), sub]
        return rcopy(ref, ref, rs.at[s, sub], rr.at[s, sub], nxt)

    def side(chip_id, sub):
        ref = g.at[chip_id, sub]
        return rcopy(ref, ref, fs.at[chip_id, sub], fr.at[chip_id, sub], sib)

    side(z, c).start()
    oref = go.at[z, c]
    o_side = rcopy(oref, oref, ofs.at[nz], ofr.at[nz], sib)
    o_side.start()
    ring(0, c).start()
    osib = go.at[z, 1 - c]
    side(z, 1 - c).wait_recv()
    ring(0, 1 - c).start()

    hv = hidden[...].astype(F32)
    power = jnp.mean(hv * hv, axis=-1, keepdims=True)
    normed[...] = (hv * lax.rsqrt(power + norm_eps) * attn_gain[...]).astype(BF16)

    def fill_prefix():
        rows, cols = nw * 16, 64
        it = iota((rows, nw), 0) // 16
        gid = jnp.sum(jnp.where(it == iota((rows, nw), 1), groups[...], 0), axis=1, keepdims=True)
        r_id = lax.rem(iota((rows, cols), 0), 16)
        c_id = iota((rows, cols), 1)
        same = lax.rem(c_id, 8) == gid
        one_k = (same & (c_id // 8 == r_id)).astype(F32).astype(BF16)
        one_v = (same & (c_id // 8 + 8 == r_id)).astype(F32).astype(BF16)
        picked = mm(one_k, pk[...].reshape(cols, HD)) + mm(one_v, pv[...].reshape(cols, HD))
        ps[...] = picked.astype(BF16).reshape(ps.shape)

    def fill_tree():
        size = parents.shape[1]
        a, b = iota((size, size), 0), iota((size, size), 1)
        eye = (a == b).astype(F32)
        up_t = jnp.maximum(eye, (parents[...] == a).astype(F32))
        for _ in range(6):
            m = up_t.astype(BF16)
            up_t = (mm(m, m) > 0.5).astype(F32)
        depth = jnp.sum(up_t, axis=0, keepdims=True) - 1.0
        full = mm(up_t.astype(BF16), eye.astype(BF16), DIMS0)
        anc[...] = full
        on_path = jnp.sum(jnp.where(a == acc_node[0], full, 0.0), axis=0, keepdims=True)
        slot = jnp.where(on_path > 0.5, lens[0] + depth.astype(jnp.int32), put.shape[0])
        put[...] = (iota(put.shape, 0) == slot).astype(F32).astype(BF16)

    def fill_slots():
        a, b = iota((tok, E), 0), iota((tok, E), 1)
        idv = ids[...]
        named = jnp.zeros((tok, E), F32)
        for k in range(idv.shape[1]):
            named = named + (idv[:, k : k + 1] == b).astype(F32)
        earlier = mm((b < a).astype(F32).astype(BF16), named.astype(BF16))
        hit = jnp.zeros(place.shape, F32)
        cols = iota(place.shape, 1)
        for k in range(idv.shape[1]):
            idk = idv[:, k : k + 1]
            rank = jnp.sum(jnp.where(idk == b, earlier, 0.0), axis=1, keepdims=True)
            t = idk * CAP + rank.astype(jnp.int32)
            tgt[k] = jnp.broadcast_to(t, tgt.shape[1:])
            hit = hit + (cols == t).astype(F32)
        place[...] = hit.astype(BF16)

    fw = gate.shape[2]

    def fill_weights(part_id):
        for i, ref in ((0, gate), (2, up)):
            for e in range(2):
                lo = part_id * 512
                wgt[lo : lo + 512, (i + e) * fw : (i + e + 1) * fw] = ref[e, lo : lo + 512, :]

    fillers = {
        1: fill_prefix, 2: fill_tree, 3: fill_slots,
        4: lambda: fill_weights(0), 5: lambda: fill_weights(1), 6: lambda: fill_weights(2), 7: lambda: fill_weights(3),
    }
    for s in range(1, nz // 2):
        for i in range(2):
            sub = c if i == 0 else 1 - c
            got(s - 1, sub).wait_recv()
            if s < nz // 2 - 1 or i == 0:
                ring(s, sub).start()
            side(chip(-sg * s), sub).start()
        fillers[s]()
    got(nz // 2 - 1, c).wait_recv()
    side(chip(nz // 2), c).start()
    for s in range(1, nz // 2):
        for sub in range(2):
            side(chip(sg * s), sub).wait_recv()
    side(chip(nz // 2), 1 - c).wait_recv()

    def psend(d, _):
        t = lax.rem(w + d, nw)
        rcopy(ps.at[t], pr.at[w], pss.at[t], psr.at[w], (t, n)).start()
        return 0

    lax.fori_loop(1, nw, psend, 0)
    cp_own = pltpu.make_async_copy(ps.at[w], pr.at[w], psr.at[w])
    cp_own.start()

    rcopy(osib, osib, ofs.at[nz], ofr.at[nz], sib).wait_recv()

    def oring(s):
        k = chip(-sg * s)
        ref = go.at[k] if s < nz // 2 - 1 else go.at[k, c]
        return rcopy(ref, ref, os.at[s], orr.at[s], nxt)

    def ogot(s):
        k = chip(-sg * (s + 1))
        ref = go.at[k] if s < nz // 2 - 1 else go.at[k, c]
        return rcopy(ref, ref, os.at[s], orr.at[s], nxt)

    def oside(s, mine):
        k = chip(-sg * s) if mine else chip(sg * s)
        ref = go.at[k] if s < nz // 2 else go.at[k, c if mine else 1 - c]
        return rcopy(ref, ref, ofs.at[k], ofr.at[k], sib)

    oring(0).start()
    scale = 1.0 / math.sqrt(HD)

    def fill_qkv(i, ref):
        def run():
            ref[...] = mm(normed[...], g[:, :, i].reshape(-1, HD)).astype(BF16)
        return run

    def fill_cache():
        pos = iota(cs.shape, 1)
        ln = lens[0]
        ok = (pos < ln) & ((pos < SINK) | (pos >= ln - WIN))
        cs[...] = jnp.where(ok, mm(qs[...], cache_k[0], DIMS1) * scale, NEG)
        ts[...] = jnp.where(anc[...] > 0.5, mm(qs[...], ks[...], DIMS1) * scale, NEG)

    def fill_compact(fresh, cache, out):
        def run():
            moved = mm(put[...], fresh[...])
            written = jnp.sum(put[...].astype(F32), axis=1, keepdims=True) > 0.5
            out[0] = jnp.where(written, moved.astype(BF16), cache[0])
        return run

    fillers = {
        1: fill_qkv(0, qs), 2: fill_qkv(1, ks), 3: fill_qkv(2, vs), 4: fill_cache,
        5: fill_compact(ks, cache_k, new_k), 6: fill_compact(vs, cache_v, new_v), 7: lambda: None,
    }
    for s in range(1, nz // 2):
        ogot(s - 1).wait_recv()
        oring(s).start()
        oside(s, True).start()
        fillers[s]()
    ogot(nz // 2 - 1).wait_recv()
    oside(nz // 2, True).start()

    cp_own.wait()

    def pwait(d, _):
        t = lax.rem(w + d, nw)
        rcopy(pr.at[t], pr.at[t], pss.at[t], psr.at[t], sib).wait_recv()
        return 0

    lax.fori_loop(1, nw, pwait, 0)
    prows = pr[...].reshape(-1, HD)
    is_key = lax.rem(iota((tok, nw * 16), 1), 16) < 8
    psc = jnp.where(is_key, mm(qs[...], prows, DIMS1) * scale, NEG)
    csc, tsc = cs[...], ts[...]
    top = jnp.maximum(
        jnp.max(psc, axis=1, keepdims=True),
        jnp.maximum(jnp.max(csc, axis=1, keepdims=True), jnp.max(tsc, axis=1, keepdims=True)),
    )
    pw = jnp.where(is_key, jnp.exp(psc - top), 0.0)
    pos = iota(cs.shape, 1)
    ok = (pos < lens[0]) & ((pos < SINK) | (pos >= lens[0] - WIN))
    cw = jnp.where(ok, jnp.exp(csc - top), 0.0)
    tw = jnp.where(anc[...] > 0.5, jnp.exp(tsc - top), 0.0)
    total = (
        jnp.sum(pw, axis=1, keepdims=True) + jnp.sum(cw, axis=1, keepdims=True) + jnp.sum(tw, axis=1, keepdims=True)
    )
    weighted = (
        mm(pltpu.roll(pw, 8, 1).astype(BF16), prows)
        + mm(cw.astype(BF16), cache_v[0])
        + mm(tw.astype(BF16), vs[...])
    )
    attended = (weighted / total).astype(BF16)
    for s in range(1, nz // 2 + 1):
        oside(s, False).wait_recv()
    for i in range(4):
        four = go[i * 4 : i * 4 + 4].reshape(512, HD)
        terms = mm(attended, four, DIMS1)
        for j in range(4):
            part[i * 4 + j] = terms[:, j * HD : (j + 1) * HD].astype(BF16)

    def send1(d, _):
        t = lax.rem(n + d, nn)
        rcopy(part.at[t], rbuf.at[n], s1.at[t], r1s.at[n], (w, t)).start()
        return 0

    lax.fori_loop(1, nn, send1, 0)
    col = pl.multiple_of(n * HD, HD)

    def add1(d, acc):
        t = lax.rem(n + d, nn)
        rcopy(rbuf.at[t], rbuf.at[t], s1.at[t], r1s.at[t], (w, t)).wait_recv()
        return acc + rbuf[t].astype(F32)

    summed = lax.fori_loop(1, nn, add1, part[n].astype(F32))
    mixed = (hidden[:, pl.ds(col, HD)].astype(F32) + summed).astype(BF16)
    mx[n] = mixed
    mf = mixed.astype(F32)
    sq = jnp.sum(mf * mf, axis=1, keepdims=True)
    eye = iota((tok, HD), 0) == iota((tok, HD), 1)
    ssb[n] = jnp.broadcast_to(jnp.sum(jnp.where(eye, sq, 0.0), axis=0, keepdims=True), (8, HD))

    def send3(d, _):
        t = lax.rem(n + d, nn)
        rcopy(ssb.at[n], ssb.at[n], s3.at[t], r3s.at[n], (w, t)).start()
        return 0

    lax.fori_loop(1, nn, send3, 0)

    def send2(d, _):
        t = lax.rem(n + d, nn)
        rcopy(mx.at[n], mx.at[n], s2.at[t], r2s.at[n], (w, t)).start()
        return 0

    lax.fori_loop(1, nn, send2, 0)

    def wait3(d, _):
        t = lax.rem(n + d, nn)
        rcopy(ssb.at[t], ssb.at[t], s3.at[t], r3s.at[t], (w, t)).wait_recv()
        return 0

    lax.fori_loop(1, nn, wait3, 0)
    sums = jnp.sum(ssb[...], axis=0)[0:1]
    sq_all = jnp.sum(jnp.where(eye, sums, 0.0), axis=1, keepdims=True)
    inv = lax.rsqrt(sq_all / (nn * HD) + norm_eps)
    mine = (mf * inv * expert_gain[:, pl.ds(col, HD)]).astype(BF16)
    slots = mm(place[...], mine, DIMS0)
    dflat = dbuf.reshape(place.shape[1], HD)
    dflat[...] = slots.astype(BF16)

    def slot_of(dz):
        return lax.rem(nz + nz // 2 - dz, nz) * 2 + c

    def send_d(dz, core):
        t = chip(dz) * 2 + core
        rcopy(dbuf.at[t], r.at[slot_of(dz)], ds.at[t], dr.at[slot_of(dz)], (t, n)).start()

    cp_d = pltpu.make_async_copy(dbuf.at[w], r.at[nz + c], dr.at[nz + c])
    cp_d.start()
    send_d(0, 1 - c)
    for k in range(1, nz // 2):
        for dz in (k, -k):
            for core in range(2):
                send_d(dz, core)
    for core in range(2):
        send_d(nz // 2, core)

    def wait2(d, _):
        t = lax.rem(n + d, nn)
        rcopy(mx.at[t], mx.at[t], s2.at[t], r2s.at[t], (w, t)).wait_recv()
        return 0

    def fill_router():
        lax.fori_loop(1, nn, wait2, 0)
        logits = jnp.zeros((tok, E), F32)
        for t in range(nn):
            row = (mx[t].astype(F32) * inv * expert_gain[:, t * HD : (t + 1) * HD]).astype(BF16)
            logits = logits + mm(row, router[t * HD : (t + 1) * HD, :])
        b = iota((tok, E), 1)
        idv = ids[...]
        picks = [
            jnp.sum(jnp.where(idv[:, k : k + 1] == b, logits, 0.0), axis=1, keepdims=True)
            for k in range(idv.shape[1])
        ]
        best = picks[0]
        for p in picks[1:]:
            best = jnp.maximum(best, p)
        exps = [jnp.exp(p - best) for p in picks]
        den = exps[0]
        for e in exps[1:]:
            den = den + e
        cols = iota(mix.shape, 1)
        m = jnp.zeros(mix.shape, F32)
        for k, e in enumerate(exps):
            m = m + jnp.where(cols == tgt[k][:, 0:1], e / den, 0.0)
        mix[...] = m

    rflat = r.reshape(place.shape[1], HD)
    size = place.shape[1] // CHUNKS
    high = size - LOW

    def dev(axis, off):
        if axis == 0:
            return (w, y * NX + lax.rem(x + off + NX, NX))
        return (w, lax.rem(y + off + NY, NY) * NX + x)

    def pos_of(axis, off):
        if axis == 0:
            return lax.rem(x + off + NX, NX)
        return lax.rem(y + off + NY, NY)

    def xref(axis, b, o, lo, ln):
        if axis == 0:
            return xs.at[o, b, pl.ds(lo, ln), :]
        return xs.at[b, o, pl.ds(lo, ln), :]

    def hop(p, slot, b_off, o_off, half, to):
        axis, lo = p % 2, ORDER[p] * size
        lo, ln = {0: (lo, size), 1: (lo, LOW), 2: (lo + LOW, high)}[half]
        ref = xref(axis, pos_of(axis, b_off), pos_of(1 - axis, o_off), lo, ln)
        return rcopy(ref, ref, ss.at[p, slot], rrs.at[p, slot], to)

    def stage0(p):
        j, axis = ORDER[p], p % 2
        for i in range(nw // CHUNKS):
            ref = r.at[j * (nw // CHUNKS) + i]
            rcopy(ref, ref, ds.at[0], dr.at[j * (nw // CHUNKS) + i], sib).wait_recv()
        xs[y, x, pl.ds(j * size, size), :] = rflat[pl.ds(j * size, size), :]
        hop(p, 0, 0, 0, 0, dev(axis, 1)).start()
        hop(p, 1, 0, 0, 0, dev(axis, -1)).start()
        hop(p, 4, 0, 0, 0, dev(1 - axis, 1)).start()
        hop(p, 5, 0, 0, 0, dev(1 - axis, -1)).start()

    def stage1(p):
        axis = p % 2
        for slot, off, half in ((0, -1, 1), (1, 1, 2)):
            hop(p, slot, off, 0, 0, sib).wait_recv()
            hop(p, slot + 2, off, 0, half, dev(axis, -off)).start()
            hop(p, 8 + 4 * slot, off, 0, 0, dev(1 - axis, 1)).start()
            hop(p, 9 + 4 * slot, off, 0, 0, dev(1 - axis, -1)).start()

    def second(p, base, b_off):
        axis = p % 2
        hop(p, base, b_off, -1, 0, sib).wait_recv()
        hop(p, base + 2, b_off, -1, 1, dev(1 - axis, 1)).start()
        hop(p, base + 1, b_off, 1, 0, sib).wait_recv()
        hop(p, base + 3, b_off, 1, 2, dev(1 - axis, -1)).start()

    def stage2(p):
        axis = p % 2
        second(p, 4, 0)
        hop(p, 2, 2, 0, 1, sib).wait_recv()
        hop(p, 3, 2, 0, 2, sib).wait_recv()
        hop(p, 16, 2, 0, 0, dev(1 - axis, 1)).start()
        hop(p, 17, 2, 0, 0, dev(1 - axis, -1)).start()
        second(p, 8, -1)
        second(p, 12, 1)

    def stage3(p):
        second(p, 16, 2)

    def sref(axis, b, lo, ln):
        if axis == 0:
            return src.at[:, b, pl.ds(lo, ln), :]
        return src.at[b, :, pl.ds(lo, ln), :]

    def val(axis, b, lo, ln):
        return sref(axis, b, lo, ln)[...].astype(F32)

    def f1d(p, slot, lo, ln, to):
        ref = f1.at[p, :, pl.ds(lo, ln), :]
        return rcopy(ref, ref, us.at[p, slot], ur.at[p, slot], to)

    def f2d(p, slot, lo, ln, to):
        ref = f2.at[p, pl.ds(lo, ln), :]
        return rcopy(ref, ref, us.at[p, slot], ur.at[p, slot], to)

    def stage4(p):
        axis, lo = p % 2, ORDER[p] * size
        for base, b_off in ((4, 0), (8, -1), (12, 1), (16, 2)):
            hop(p, base + 2, b_off, 2, 1, sib).wait_recv()
            hop(p, base + 3, b_off, 2, 2, sib).wait_recv()
        units = jnp.zeros((size, 4 * fw), F32)
        for t in range(nn):
            units = units + mm(xs[t // NX, t % NX, lo : lo + size, :], wgt[t * HD : (t + 1) * HD, :])
        gt = units[:, : 2 * fw]
        act = gt / (1.0 + jnp.exp(-gt)) * units[:, 2 * fw :]
        row = lax.rem(iota(act.shape, 0), 2 * CAP)
        keep = (row >= CAP) == (iota(act.shape, 1) >= fw)
        act = jnp.where(keep, act, 0.0).astype(BF16)
        dn = down[...].reshape(2 * fw, -1)
        for t in range(nn):
            src[t // NX, t % NX, lo : lo + size, :] = mm(act, dn[:, t * HD : (t + 1) * HD]).astype(BF16)
        b2 = pos_of(axis, 2)
        rcopy(sref(axis, b2, lo, LOW), f1.at[p, :, pl.ds(0, LOW), :], us.at[p, 0], ur.at[p, 0], dev(axis, 1)).start()
        rcopy(
            sref(axis, b2, lo + LOW, high), f1.at[p, :, pl.ds(LOW, high), :], us.at[p, 1], ur.at[p, 1], dev(axis, -1)
        ).start()

    def t1d(p, k, to):
        return rcopy(t1.at[p, k], r1.at[p, k], us.at[p, 2 + k], ur.at[p, 2 + k], to)

    def t2d(p, k, to):
        return rcopy(t2.at[p, k], r2.at[p, k], us.at[p, 6 + k], ur.at[p, 6 + k], to)

    def stage5(p):
        axis, lo = p % 2, ORDER[p] * size
        bp, bm = pos_of(axis, 1), pos_of(axis, -1)
        t1[p, 0, :, LOW:, :] = sref(axis, bp, lo + LOW, high)[...]
        t1[p, 1, :, :LOW, :] = sref(axis, bm, lo, LOW)[...]
        f1d(p, 0, 0, LOW, sib).wait_recv()
        t1[p, 0, :, :LOW, :] = (val(axis, bp, lo, LOW) + f1[p, :, :LOW, :].astype(F32)).astype(BF16)
        t1d(p, 0, dev(axis, 1)).start()
        f1d(p, 1, LOW, high, sib).wait_recv()
        t1[p, 1, :, LOW:, :] = (val(axis, bm, lo + LOW, high) + f1[p, :, LOW:, :].astype(F32)).astype(BF16)
        t1d(p, 1, dev(axis, -1)).start()

    def stage6(p):
        axis, lo = p % 2, ORDER[p] * size
        t1d(p, 0, sib).wait_recv()
        t1d(p, 1, sib).wait_recv()
        m2[p] = (val(axis, pos_of(axis, 0), lo, size) + r1[p, 0].astype(F32) + r1[p, 1].astype(F32)).astype(BF16)
        b2 = pos_of(1 - axis, 2)
        rcopy(m2.at[p, b2, pl.ds(0, LOW), :], f2.at[p, pl.ds(0, LOW), :], us.at[p, 4], ur.at[p, 4], dev(1 - axis, 1)).start()
        rcopy(
            m2.at[p, b2, pl.ds(LOW, high), :], f2.at[p, pl.ds(LOW, high), :], us.at[p, 5], ur.at[p, 5], dev(1 - axis, -1)
        ).start()

    def stage7(p):
        axis = p % 2
        bp, bm = pos_of(1 - axis, 1), pos_of(1 - axis, -1)
        t2[p, 0, LOW:, :] = m2[p, bp, LOW:, :]
        t2[p, 1, :LOW, :] = m2[p, bm, :LOW, :]
        f2d(p, 4, 0, LOW, sib).wait_recv()
        t2[p, 0, :LOW, :] = (m2[p, bp, :LOW, :].astype(F32) + f2[p, :LOW, :].astype(F32)).astype(BF16)
        t2d(p, 0, dev(1 - axis, 1)).start()
        f2d(p, 5, LOW, high, sib).wait_recv()
        t2[p, 1, LOW:, :] = (m2[p, bm, LOW:, :].astype(F32) + f2[p, LOW:, :].astype(F32)).astype(BF16)
        t2d(p, 1, dev(1 - axis, -1)).start()

    bflat = bbuf.reshape(place.shape[1], HD)

    def stage8(p):
        j, axis = ORDER[p], p % 2
        t2d(p, 0, sib).wait_recv()
        t2d(p, 1, sib).wait_recv()
        bflat[pl.ds(j * size, size), :] = (
            m2[p, pos_of(1 - axis, 0)].astype(F32) + r2[p, 0].astype(F32) + r2[p, 1].astype(F32)
        ).astype(BF16)
        for i in range(nz // CHUNKS):
            rel = j * (nz // CHUNKS) + i
            for core in range(2):
                t = chip(rel - nz // 2) * 2 + core
                a = bbuf.at[rel * 2 + core]
                if rel == nz // 2:
                    if core == 0:
                        pltpu.make_async_copy(bbuf.at[nz + c], bk.at[w], er.at[w]).start()
                        rcopy(bbuf.at[nz + 1 - c], bk.at[w], es.at[nz + 1 - c], er.at[w], sib).start()
                else:
                    rcopy(a, bk.at[w], es.at[rel * 2 + core], er.at[w], (t, n)).start()

    stages = (stage0, stage1, stage2, stage3, stage4, stage5, stage6, stage7, stage8)
    for t in range(CHUNKS + len(stages) - 1):
        for k in reversed(range(len(stages))):
            if 0 <= t - k < CHUNKS:
                stages[k](t - k)
        if t == 0:
            fill_router()

    def wait_b(d, _):
        t = lax.rem(w + d, nw)
        rcopy(bk.at[t], bk.at[t], es.at[t], er.at[t], sib).wait_recv()
        return 0

    lax.fori_loop(0, nw, wait_b, 0)
    moe = lax.dot_general(
        mix[...], bk.reshape(place.shape[1], HD)[...].astype(F32), (((1,), (0,)), ((), ())),
        precision=lax.Precision.HIGHEST, preferred_element_type=F32,
    )
    layer_out[...] = (mx[n].astype(F32) + moe).astype(BF16)

    for s in range(nz // 2):
        for i in range(2):
            if s < nz // 2 - 1 or i == 0:
                ring(s, c if i == 0 else 1 - c).wait_send()
        oring(s).wait_send()
    side(z, c).wait_send()
    o_side.wait_send()
    for s in range(1, nz // 2):
        for sub in range(2):
            side(chip(-sg * s), sub).wait_send()
        oside(s, True).wait_send()
    side(chip(nz // 2), c).wait_send()
    oside(nz // 2, True).wait_send()

    def sent_w(d, _):
        t = lax.rem(w + d, nw)
        rcopy(ps.at[t], pr.at[w], pss.at[t], psr.at[w], sib).wait_send()
        rcopy(dbuf.at[t], r.at[0], ds.at[t], dr.at[0], sib).wait_send()
        return 0

    lax.fori_loop(1, nw, sent_w, 0)

    def sent_b(d, _):
        t = lax.rem(nz + c + d, nw)
        rcopy(bbuf.at[t], bk.at[w], es.at[t], er.at[w], sib).wait_send()
        return 0

    lax.fori_loop(1, nw, sent_b, 0)

    def sent_n(d, _):
        t = lax.rem(n + d, nn)
        rcopy(part.at[t], rbuf.at[n], s1.at[t], r1s.at[n], sib).wait_send()
        rcopy(ssb.at[n], ssb.at[n], s3.at[t], r3s.at[n], sib).wait_send()
        rcopy(mx.at[n], mx.at[n], s2.at[t], r2s.at[n], sib).wait_send()
        return 0

    lax.fori_loop(1, nn, sent_n, 0)
    for p in range(CHUNKS):
        for slot in range(20):
            half = 0 if slot < 2 or slot % 4 < 2 else slot % 4 - 1
            hop(p, slot, 0, 0, half, sib).wait_send()
        f1d(p, 0, 0, LOW, sib).wait_send()
        f1d(p, 1, LOW, high, sib).wait_send()
        f2d(p, 4, 0, LOW, sib).wait_send()
        f2d(p, 5, LOW, high, sib).wait_send()
        for k in range(2):
            t1d(p, k, sib).wait_send()
            t2d(p, k, sib).wait_send()


def body(
    hidden, attn_gain, expert_gain, query_weight, key_weight, value_weight, output_weight, router_weight,
    gate_weight, up_weight, down_weight, prefix_keys, prefix_values, cache_keys, cache_values, parents,
    cache_lengths, group_ids, expert_ids, accepted,
):
    tok, width = hidden.shape
    nn = lax.axis_size("narrow")
    nw = lax.axis_size("wide")
    nz = nw // 2
    rows = nw * gate_weight.shape[0] * CAP
    size = rows // CHUNKS
    cache = cache_keys.shape[1]
    vm = pl.BlockSpec(memory_space=pltpu.VMEM)
    sm = pl.BlockSpec(memory_space=pltpu.SMEM)
    dma = pltpu.SemaphoreType.DMA

    def v(*shape, t=BF16):
        return pltpu.VMEM(shape, t)

    pair = rows // nw // 2
    scratch = [
        v(tok, width), v(nz, 2, 3, 64, HD), v(nz, 2, 64, HD), v(nw, 16, HD), v(nw, 16, HD),
        v(tok, HD), v(tok, HD), v(tok, HD), v(tok, cache, t=F32), v(tok, tok, t=F32), v(tok, tok, t=F32),
        v(cache, tok), v(nn, tok, HD), v(nn, tok, HD), v(nn, tok, HD), v(nn, 8, HD, t=F32),
        v(width, 4 * gate_weight.shape[2]), v(expert_ids.shape[1], tok, HD, t=jnp.int32), v(tok, rows), v(tok, rows, t=F32),
        v(nw, pair, 2, HD), v(nw, pair, 2, HD), v(NY, NX, rows, HD), v(NY, NX, rows, HD),
        v(CHUNKS, 2, 4, size, HD), v(CHUNKS, 4, size, HD), v(CHUNKS, 2, 4, size, HD), v(CHUNKS, 4, size, HD),
        v(CHUNKS, 2, size, HD), v(CHUNKS, size, HD), v(CHUNKS, 2, size, HD), v(nw, pair, 2, HD), v(nw, pair, 2, HD),
        dma((4,)), dma((nz // 2, 2)), dma((nz // 2, 2)), dma((nz, 2)), dma((nz, 2)),
        dma((nz // 2,)), dma((nz // 2,)), dma((nz + 1,)), dma((nz + 1,)), dma((nw,)), dma((nw,)),
        dma((nn,)), dma((nn,)), dma((nn,)), dma((nn,)), dma((nn,)), dma((nn,)), dma((nw,)), dma((nw,)),
        dma((CHUNKS, 20)), dma((CHUNKS, 20)), dma((CHUNKS, 8)), dma((CHUNKS, 8)), dma((nw,)), dma((nw,)),
    ]
    return pl.pallas_call(
        layer_kernel,
        out_shape=(
            jax.ShapeDtypeStruct((tok, HD), BF16),
            jax.ShapeDtypeStruct(cache_keys.shape, BF16),
            jax.ShapeDtypeStruct(cache_values.shape, BF16),
        ),
        in_specs=[sm, sm] + [vm] * 18,
        out_specs=(vm, vm, vm),
        scratch_shapes=scratch,
        compiler_params=pltpu.CompilerParams(
            collective_id=0, has_side_effects=True, vmem_limit_bytes=60 * 1024 * 1024
        ),
        name="layer",
    )(
        cache_lengths, accepted, hidden, attn_gain[None], expert_gain[None], query_weight, key_weight, value_weight,
        output_weight, router_weight, gate_weight, up_weight, down_weight, prefix_keys, prefix_values,
        cache_keys, cache_values, parents, group_ids[None], expert_ids,
    )


def solution(mesh):
    in_specs = (
        P("wide", None),
        P(),
        P(),
        P("wide", "narrow"),
        P("wide", "narrow"),
        P("wide", "narrow"),
        P("wide", "narrow"),
        P(),
        P("wide", None, "narrow"),
        P("wide", None, "narrow"),
        P("wide", "narrow", None),
        P("wide", None, "narrow"),
        P("wide", None, "narrow"),
        P("wide", None, "narrow"),
        P("wide", None, "narrow"),
        P("wide", None),
        P("wide"),
        P(),
        P("wide", None),
        P("wide"),
    )
    out_specs = (P("wide", "narrow"), P("wide", None, "narrow"), P("wide", None, "narrow"))
    return jax.shard_map(body, mesh=mesh, in_specs=in_specs, out_specs=out_specs, check_vma=False)
```

time: 690 us -> 167 us (0.24)
  blocking collectives: 311 us -> 0 us
  waiting for transfers between devices: 292 us -> 0 us
  Pallas kernels: 0 us -> 155 us
  local copies, waits for them, and re-layouts: 39.5 us -> 9.76 us
  between operations: 17.8 us -> 2 us
  matrix products: 12.3 us -> 0 us
  other arithmetic: 12.3 us -> 0 us
    all_gather x6 -> x0, blocking collectives: 184 us -> none  [the longest x1 39 us: body(): lax.all_gather(prefix_values, 'wide', axis=0, tiled=True)]
    pallas_call x0 -> x1, Pallas kernels: none -> 155 us  [body(): pl.pallas_call(layer_kernel, out_shape=(jax.ShapeDtypeStruct((tok, HD), B...]
    all_to_all x1 -> x0, blocking collectives: 127 us -> none  [body(): lax.all_to_all(send_rows, 'wide', split_axis=0, concat_axis=0, tiled=True)]
    psum x1 -> x0, waiting for transfers between devices: 109 us -> none  [body(): summed = lax.psum(partial_value, 'narrow')]
    all_to_all x1 -> x0, waiting for transfers between devices: 108 us -> none  [body(): lax.all_to_all(produced, 'wide', split_axis=0, concat_axis=0, tiled=True)]
    reduce_scatter x1 -> x0, waiting for transfers between devices: 75.3 us -> none  [body(): lax.psum_scatter(partial_moe, 'narrow', scatter_dimension=1, tiled=True)]
    dot_general x19 -> x0, matrix products: 12.3 us -> none  [the longest x1 4.06 us: body(): jnp.einsum('secf,efd->secd', activated, down_weight, preferred_element_ty...]
    reshape x3 -> x0, local copies, waits for them, and re-layouts: 11 us -> none  [the longest x2 7.64 us: body(): send_rows = send_rows.reshape(wide_count, exp_local, CAP, model_width)]
  transfers between devices with their start and end apart: 3 -> 0, of which waited for: 3 -> 0; matrix products, arithmetic and copies ran while one was open for 1% -> 0% of each run, Pallas kernels for 0% -> 0%
where the time goes in v2:
time: 167 us; the launch traced here: 166 us
  Pallas kernels  155 us (93%)
  local copies, waits for them, and re-layouts  9.76 us (6%)
  between operations  2 us (1%)
    pallas_call x1, Pallas kernels, body(): pl.pallas_call(layer_kernel, out_shape=(jax.ShapeDtypeStruct((tok, HD), B...  155 us
    unnamed x13, local copies, waits for them, and re-layouts  9.76 us

profile of v2, /device:TPU:1, one launch (start us, length us, event | category | flops | bytes accessed | tf_op | source)
XLA Modules:
  0.0 166.4 jit_solution(18428051715012386957)
XLA Ops:
  0.6 0.0 copy-start
  2.0 1.4 copy.26.ids
  3.4 2.0 %copy.23.router = bf16[2048,64]{1,0:T(8,128)(2,1)} copy(bf16[2048,64]{0,1:T(8,128)(2,1)} %param.27) | data formatting | bytes 524288 | tf_op args[7]
  5.3 0.0 copy-done
  5.3 0.0 copy-start.1
  5.3 1.3 copy.24.gate
  6.6 0.0 copy-done.1
  6.7 1.4 copy.25.up
  8.0 154.7 %layer.1 = (bf16[64,128]{1,0:T(8,128)(2,1)}, bf16[1,1024,128]{2,1,0:T(8,128)(2,1)}, bf16[1,1024,128]{2,1,0:T(8,128)(2,1)}) custom-call(s32[1]{0:T(128)S(6)} %copy.30.lens, s32[1]{0:T(128)S(6)} %copy.31.acc_node, bf16[64,2048]{1,0:T(8,128)(2,1)} %hidden.1, f32[1,2048]{1,0:T(1,128)} %bitcast.3, f32[1,2048]{1,0:T(1,128)} %bitcast.4, bf16[64,128]{1,0:T(8,128)(2,1)} %q_in.1, ...), custom_call_target="tpu_custom_call" | custom-call | tf_op jit(solution)/shard_map/layer/pallas_call | solution.py:655
  162.7 1.3 copy.32
  164.0 0.0 copy-start.2
  164.0 1.7 %copy.33 = bf16[1,1024,128]{2,1,0:T(8,128)(2,1)} copy(bf16[1,1024,128]{2,1,0:T(8,128)(2,1)} %get-tuple-element.7) | data formatting | bytes 524288
  165.7 0.0 copy-done.2
  165.7 0.7 copy.34
Async XLA Ops:
  0.6 4.7 %copy-start = (bf16[2,2048,64]{1,2,0:T(8,128)(2,1)S(1)}, bf16[2,2048,64]{1,2,0:T(8,128)(2,1)}, u32[]{:S(2)}) copy-start(bf16[2,2048,64]{1,2,0:T(8,128)(2,1)} %param.28) | copy-start | bytes 1572868
  5.3 1.3 copy-start.1
  164.0 1.7 %copy-start.2 = (bf16[1,1024,128]{2,1,0:T(8,128)(2,1)S(1)}, bf16[1,1024,128]{2,1,0:T(8,128)(2,1)}, u32[]{:S(2)}) copy-start(bf16[1,1024,128]{2,1,0:T(8,128)(2,1)} %get-tuple-element.8) | copy-start | bytes 786436

commit v3 on v2

--- a/solution.py
+++ b/solution.py
@@ -50,12 +50,13 @@
 
 
 def layer_kernel(
-    lens, acc_node, hidden, attn_gain, expert_gain, q_in, k_in, v_in, o_in, router, gate, up, down,
-    pk, pv, cache_k, cache_v, parents, groups, ids,
+    lens, acc_node, attn_gain, expert_gain, parents, groups, ids,
+    hidden_in, q_in, k_in, v_in, o_in, router_in, gate, up, down, pk_in, pv_in, ck_in, cv_in,
     layer_out, new_k, new_v,
-    normed, g, go, ps, pr, qs, ks, vs, cs, ts, anc, put, part, rbuf, mx, ssb, wgt, tgt, place, mix,
+    hidden, router, wgt, dn, cache_k, cache_v, pk, pv, proj,
+    normed, g, go, ps, pr, qs, ks, vs, cs, ts, anc, put, part, rbuf, mx, tgt, place, mix,
     dbuf, r, xs, src, r1, f1, t1, m2, r2, f2, t2, bbuf, bk,
-    ls, rs, rr, fs, fr, os, orr, ofs, ofr, pss, psr, s1, r1s, s2, r2s, s3, r3s, ds, dr, ss, rrs, us, ur, es, er,
+    ls, rs, rr, fs, fr, os, orr, ofs, ofr, pss, psr, s1, r1s, s2, r2s, ds, dr, ss, rrs, us, ur, es, er,
 ):
     nz, nn, nw = g.shape[0], part.shape[0], pr.shape[0]
     tok = hidden.shape[0]
@@ -83,15 +84,18 @@
         return 0
 
     lax.fori_loop(1, nn, greet, 0)
-    local = [
-        pltpu.make_async_copy(a, b, ls.at[i])
-        for i, (a, b) in enumerate(
-            ((q_in, g.at[z, c, 0]), (k_in, g.at[z, c, 1]), (v_in, g.at[z, c, 2]), (o_in, go.at[z, c]))
-        )
-    ]
+    fw = gate.shape[1]
+    moves = (
+        (q_in, g.at[z, c, 0]), (k_in, g.at[z, c, 1]), (v_in, g.at[z, c, 2]), (o_in, go.at[z, c]),
+        (hidden_in, hidden), (pk_in, pk), (pv_in, pv), (ck_in.at[0], cache_k), (cv_in.at[0], cache_v),
+        (gate.at[0], wgt.at[pl.ds(0, fw), :]), (gate.at[1], wgt.at[pl.ds(fw, fw), :]),
+        (up.at[0], wgt.at[pl.ds(2 * fw, fw), :]), (up.at[1], wgt.at[pl.ds(3 * fw, fw), :]),
+        (down.at[0], dn.at[pl.ds(0, fw), :]), (down.at[1], dn.at[pl.ds(fw, fw), :]), (router_in, router),
+    )
+    local = [pltpu.make_async_copy(a, b, ls.at[i]) for i, (a, b) in enumerate(moves)]
     for cp in local:
         cp.start()
-    for cp in local:
+    for cp in local[:4]:
         cp.wait()
     pl.semaphore_wait(barrier, nn + 2)
 
@@ -116,11 +120,15 @@
     side(z, 1 - c).wait_recv()
     ring(0, 1 - c).start()
 
+    local[4].wait()
     hv = hidden[...].astype(F32)
     power = jnp.mean(hv * hv, axis=-1, keepdims=True)
     normed[...] = (hv * lax.rsqrt(power + norm_eps) * attn_gain[...]).astype(BF16)
+    proj[...] = jnp.zeros_like(proj)
 
     def fill_prefix():
+        local[5].wait()
+        local[6].wait()
         rows, cols = nw * 16, 64
         it = iota((rows, nw), 0) // 16
         gid = jnp.sum(jnp.where(it == iota((rows, nw), 1), groups[...], 0), axis=1, keepdims=True)
@@ -148,34 +156,56 @@
         put[...] = (iota(put.shape, 0) == slot).astype(F32).astype(BF16)
 
     def fill_slots():
-        a, b = iota((tok, E), 0), iota((tok, E), 1)
-        idv = ids[...]
-        named = jnp.zeros((tok, E), F32)
-        for k in range(idv.shape[1]):
-            named = named + (idv[:, k : k + 1] == b).astype(F32)
-        earlier = mm((b < a).astype(F32).astype(BF16), named.astype(BF16))
+        a, b = iota((E, tok), 0), iota((E, tok), 1)
+        named = jnp.zeros((E, tok), F32)
+        for k in range(ids.shape[0]):
+            named = named + (ids[k : k + 1, :] == a).astype(F32)
+        earlier = mm(named.astype(BF16), (iota((tok, tok), 0) < iota((tok, tok), 1)).astype(F32).astype(BF16))
         hit = jnp.zeros(place.shape, F32)
-        cols = iota(place.shape, 1)
-        for k in range(idv.shape[1]):
-            idk = idv[:, k : k + 1]
-            rank = jnp.sum(jnp.where(idk == b, earlier, 0.0), axis=1, keepdims=True)
+        rows = iota(place.shape, 0)
+        for k in range(ids.shape[0]):
+            idk = ids[k : k + 1, :]
+            rank = jnp.sum(jnp.where(idk == a, earlier, 0.0), axis=0, keepdims=True)
             t = idk * CAP + rank.astype(jnp.int32)
-            tgt[k] = jnp.broadcast_to(t, tgt.shape[1:])
-            hit = hit + (cols == t).astype(F32)
+            tgt[k : k + 1, :] = t
+            hit = hit + (rows == t).astype(F32)
         place[...] = hit.astype(BF16)
 
-    fw = gate.shape[2]
-
-    def fill_weights(part_id):
-        for i, ref in ((0, gate), (2, up)):
-            for e in range(2):
-                lo = part_id * 512
-                wgt[lo : lo + 512, (i + e) * fw : (i + e + 1) * fw] = ref[e, lo : lo + 512, :]
-
-    fillers = {
-        1: fill_prefix, 2: fill_tree, 3: fill_slots,
-        4: lambda: fill_weights(0), 5: lambda: fill_weights(1), 6: lambda: fill_weights(2), 7: lambda: fill_weights(3),
-    }
+    def oring(s):
+        k = chip(-sg * s)
+        ref = go.at[k] if s < nz // 2 - 1 else go.at[k, c]
+        return rcopy(ref, ref, os.at[s], orr.at[s], nxt)
+
+    def ogot(s):
+        k = chip(-sg * (s + 1))
+        ref = go.at[k] if s < nz // 2 - 1 else go.at[k, c]
+        return rcopy(ref, ref, os.at[s], orr.at[s], nxt)
+
+    def oside(s, mine):
+        k = chip(-sg * s) if mine else chip(sg * s)
+        ref = go.at[k] if s < nz // 2 else go.at[k, c if mine else 1 - c]
+        return rcopy(ref, ref, ofs.at[k], ofr.at[k], sib)
+
+    def send_prefix(k):
+        for core in range(2):
+            t = k * 2 + core
+            rcopy(ps.at[t], pr.at[w], pss.at[t], psr.at[w], (t, n)).start()
+
+    def project(k):
+        cols = pl.ds(pl.multiple_of(k * HD, HD), HD)
+        a = normed[:, cols]
+        for i in range(3):
+            b = jnp.concatenate([g[k, 0, i], g[k, 1, i]], axis=0)
+            proj[:, i * HD : (i + 1) * HD] += mm(a, b)
+
+    fill_prefix()
+    rcopy(osib, osib, ofs.at[nz], ofr.at[nz], sib).wait_recv()
+    oring(0).start()
+    cp_own = pltpu.make_async_copy(ps.at[w], pr.at[w], psr.at[w])
+    cp_own.start()
+    rcopy(ps.at[sib_w], pr.at[w], pss.at[sib_w], psr.at[w], sib).start()
+    project(z)
+    fillers = {1: fill_tree, 2: fill_slots}
     for s in range(1, nz // 2):
         for i in range(2):
             sub = c if i == 0 else 1 - c
@@ -183,73 +213,55 @@
             if s < nz // 2 - 1 or i == 0:
                 ring(s, sub).start()
             side(chip(-sg * s), sub).start()
-        fillers[s]()
-    got(nz // 2 - 1, c).wait_recv()
-    side(chip(nz // 2), c).start()
-    for s in range(1, nz // 2):
-        for sub in range(2):
-            side(chip(sg * s), sub).wait_recv()
-    side(chip(nz // 2), 1 - c).wait_recv()
-
-    def psend(d, _):
-        t = lax.rem(w + d, nw)
-        rcopy(ps.at[t], pr.at[w], pss.at[t], psr.at[w], (t, n)).start()
-        return 0
-
-    lax.fori_loop(1, nw, psend, 0)
-    cp_own = pltpu.make_async_copy(ps.at[w], pr.at[w], psr.at[w])
-    cp_own.start()
-
-    rcopy(osib, osib, ofs.at[nz], ofr.at[nz], sib).wait_recv()
-
-    def oring(s):
-        k = chip(-sg * s)
-        ref = go.at[k] if s < nz // 2 - 1 else go.at[k, c]
-        return rcopy(ref, ref, os.at[s], orr.at[s], nxt)
-
-    def ogot(s):
-        k = chip(-sg * (s + 1))
-        ref = go.at[k] if s < nz // 2 - 1 else go.at[k, c]
-        return rcopy(ref, ref, os.at[s], orr.at[s], nxt)
-
-    def oside(s, mine):
-        k = chip(-sg * s) if mine else chip(sg * s)
-        ref = go.at[k] if s < nz // 2 else go.at[k, c if mine else 1 - c]
-        return rcopy(ref, ref, ofs.at[k], ofr.at[k], sib)
-
-    oring(0).start()
-    scale = 1.0 / math.sqrt(HD)
-
-    def fill_qkv(i, ref):
-        def run():
-            ref[...] = mm(normed[...], g[:, :, i].reshape(-1, HD)).astype(BF16)
-        return run
-
-    def fill_cache():
-        pos = iota(cs.shape, 1)
-        ln = lens[0]
-        ok = (pos < ln) & ((pos < SINK) | (pos >= ln - WIN))
-        cs[...] = jnp.where(ok, mm(qs[...], cache_k[0], DIMS1) * scale, NEG)
-        ts[...] = jnp.where(anc[...] > 0.5, mm(qs[...], ks[...], DIMS1) * scale, NEG)
-
-    def fill_compact(fresh, cache, out):
-        def run():
-            moved = mm(put[...], fresh[...])
-            written = jnp.sum(put[...].astype(F32), axis=1, keepdims=True) > 0.5
-            out[0] = jnp.where(written, moved.astype(BF16), cache[0])
-        return run
-
-    fillers = {
-        1: fill_qkv(0, qs), 2: fill_qkv(1, ks), 3: fill_qkv(2, vs), 4: fill_cache,
-        5: fill_compact(ks, cache_k, new_k), 6: fill_compact(vs, cache_v, new_v), 7: lambda: None,
-    }
-    for s in range(1, nz // 2):
         ogot(s - 1).wait_recv()
         oring(s).start()
         oside(s, True).start()
-        fillers[s]()
+        send_prefix(chip(-sg * s))
+        if s > 1:
+            for sub in range(2):
+                side(chip(sg * (s - 1)), sub).wait_recv()
+            send_prefix(chip(sg * (s - 1)))
+            project(chip(sg * (s - 1)))
+        project(chip(-sg * s))
+        if s in fillers:
+            fillers[s]()
+    got(nz // 2 - 1, c).wait_recv()
+    side(chip(nz // 2), c).start()
     ogot(nz // 2 - 1).wait_recv()
     oside(nz // 2, True).start()
+    for sub in range(2):
+        side(chip(sg * (nz // 2 - 1)), sub).wait_recv()
+    send_prefix(chip(sg * (nz // 2 - 1)))
+    side(chip(nz // 2), 1 - c).wait_recv()
+    send_prefix(chip(nz // 2))
+    project(chip(sg * (nz // 2 - 1)))
+    project(chip(nz // 2))
+    for i, ref in enumerate((qs, ks, vs)):
+        ref[...] = proj[:, i * HD : (i + 1) * HD].astype(BF16)
+
+    def drain_ring():
+        for s in range(nz // 2):
+            for i in range(2):
+                if s < nz // 2 - 1 or i == 0:
+                    ring(s, c if i == 0 else 1 - c).wait_send()
+        side(z, c).wait_send()
+        o_side.wait_send()
+        for s in range(1, nz // 2):
+            for sub in range(2):
+                side(chip(-sg * s), sub).wait_send()
+        side(chip(nz // 2), c).wait_send()
+
+    scale = 1.0 / math.sqrt(HD)
+    local[7].wait()
+    pos = iota(cs.shape, 1)
+    ok = (pos < lens[0]) & ((pos < SINK) | (pos >= lens[0] - WIN))
+    cs[...] = jnp.where(ok, mm(qs[...], cache_k[...], DIMS1) * scale, NEG)
+    ts[...] = jnp.where(anc[...] > 0.5, mm(qs[...], ks[...], DIMS1) * scale, NEG)
+
+    def compact(fresh, cache, out):
+        moved = mm(put[...], fresh[...])
+        written = jnp.sum(put[...].astype(F32), axis=1, keepdims=True) > 0.5
+        out[0] = jnp.where(written, moved.astype(BF16), cache[...])
 
     cp_own.wait()
 
@@ -259,6 +271,19 @@
         return 0
 
     lax.fori_loop(1, nw, pwait, 0)
+    def drain_out():
+        for s in range(nz // 2):
+            oring(s).wait_send()
+        for s in range(1, nz // 2 + 1):
+            oside(s, True).wait_send()
+
+        def sent_p(d, _):
+            t = lax.rem(w + d, nw)
+            rcopy(ps.at[t], pr.at[w], pss.at[t], psr.at[w], sib).wait_send()
+            return 0
+
+        lax.fori_loop(1, nw, sent_p, 0)
+
     prows = pr[...].reshape(-1, HD)
     is_key = lax.rem(iota((tok, nw * 16), 1), 16) < 8
     psc = jnp.where(is_key, mm(qs[...], prows, DIMS1) * scale, NEG)
@@ -275,9 +300,10 @@
     total = (
         jnp.sum(pw, axis=1, keepdims=True) + jnp.sum(cw, axis=1, keepdims=True) + jnp.sum(tw, axis=1, keepdims=True)
     )
+    local[8].wait()
     weighted = (
         mm(pltpu.roll(pw, 8, 1).astype(BF16), prows)
-        + mm(cw.astype(BF16), cache_v[0])
+        + mm(cw.astype(BF16), cache_v[...])
         + mm(tw.astype(BF16), vs[...])
     )
     attended = (weighted / total).astype(BF16)
@@ -305,38 +331,19 @@
     summed = lax.fori_loop(1, nn, add1, part[n].astype(F32))
     mixed = (hidden[:, pl.ds(col, HD)].astype(F32) + summed).astype(BF16)
     mx[n] = mixed
-    mf = mixed.astype(F32)
-    sq = jnp.sum(mf * mf, axis=1, keepdims=True)
-    eye = iota((tok, HD), 0) == iota((tok, HD), 1)
-    ssb[n] = jnp.broadcast_to(jnp.sum(jnp.where(eye, sq, 0.0), axis=0, keepdims=True), (8, HD))
-
-    def send3(d, _):
-        t = lax.rem(n + d, nn)
-        rcopy(ssb.at[n], ssb.at[n], s3.at[t], r3s.at[n], (w, t)).start()
-        return 0
-
-    lax.fori_loop(1, nn, send3, 0)
-
-    def send2(d, _):
-        t = lax.rem(n + d, nn)
-        rcopy(mx.at[n], mx.at[n], s2.at[t], r2s.at[n], (w, t)).start()
-        return 0
-
-    lax.fori_loop(1, nn, send2, 0)
-
-    def wait3(d, _):
-        t = lax.rem(n + d, nn)
-        rcopy(ssb.at[t], ssb.at[t], s3.at[t], r3s.at[t], (w, t)).wait_recv()
-        return 0
-
-    lax.fori_loop(1, nn, wait3, 0)
-    sums = jnp.sum(ssb[...], axis=0)[0:1]
-    sq_all = jnp.sum(jnp.where(eye, sums, 0.0), axis=1, keepdims=True)
-    inv = lax.rsqrt(sq_all / (nn * HD) + norm_eps)
-    mine = (mf * inv * expert_gain[:, pl.ds(col, HD)]).astype(BF16)
-    slots = mm(place[...], mine, DIMS0)
-    dflat = dbuf.reshape(place.shape[1], HD)
+    slots = mm(place[...], mixed)
+    dflat = dbuf.reshape(place.shape[0], HD)
     dflat[...] = slots.astype(BF16)
+
+
+    def drain_plane():
+        def sent_n(d, _):
+            t = lax.rem(n + d, nn)
+            rcopy(part.at[t], rbuf.at[n], s1.at[t], r1s.at[n], sib).wait_send()
+            rcopy(mx.at[n], mx.at[n], s2.at[t], r2s.at[n], sib).wait_send()
+            return 0
+
+        lax.fori_loop(1, nn, sent_n, 0)
 
     def slot_of(dz):
         return lax.rem(nz + nz // 2 - dz, nz) * 2 + c
@@ -354,6 +361,14 @@
                 send_d(dz, core)
     for core in range(2):
         send_d(nz // 2, core)
+    def send2(d, _):
+        t = lax.rem(n + d, nn)
+        rcopy(mx.at[n], mx.at[n], s2.at[t], r2s.at[n], (w, t)).start()
+        return 0
+
+    lax.fori_loop(1, nn, send2, 0)
+    compact(ks, cache_k, new_k)
+    compact(vs, cache_v, new_v)
 
     def wait2(d, _):
         t = lax.rem(n + d, nn)
@@ -362,15 +377,20 @@
 
     def fill_router():
         lax.fori_loop(1, nn, wait2, 0)
-        logits = jnp.zeros((tok, E), F32)
+        local[15].wait()
+        power = jnp.zeros((tok, 1), F32)
+        for t in range(nn):
+            m = mx[t].astype(F32)
+            power = power + jnp.sum(m * m, axis=1, keepdims=True)
+        inv = lax.rsqrt(power / (nn * HD) + norm_eps)
+        logits = jnp.zeros((E, tok), F32)
         for t in range(nn):
             row = (mx[t].astype(F32) * inv * expert_gain[:, t * HD : (t + 1) * HD]).astype(BF16)
-            logits = logits + mm(row, router[t * HD : (t + 1) * HD, :])
-        b = iota((tok, E), 1)
-        idv = ids[...]
+            logits = logits + mm(router[:, t * HD : (t + 1) * HD], row, DIMS1)
+        a = iota((E, tok), 0)
         picks = [
-            jnp.sum(jnp.where(idv[:, k : k + 1] == b, logits, 0.0), axis=1, keepdims=True)
-            for k in range(idv.shape[1])
+            jnp.sum(jnp.where(ids[k : k + 1, :] == a, logits, 0.0), axis=0, keepdims=True)
+            for k in range(ids.shape[0])
         ]
         best = picks[0]
         for p in picks[1:]:
@@ -379,14 +399,22 @@
         den = exps[0]
         for e in exps[1:]:
             den = den + e
-        cols = iota(mix.shape, 1)
+        rows = iota(mix.shape, 0)
         m = jnp.zeros(mix.shape, F32)
         for k, e in enumerate(exps):
-            m = m + jnp.where(cols == tgt[k][:, 0:1], e / den, 0.0)
+            m = m + jnp.where(rows == tgt[k : k + 1, :], e / den, 0.0)
         mix[...] = m
 
-    rflat = r.reshape(place.shape[1], HD)
-    size = place.shape[1] // CHUNKS
+    def drain_dispatch():
+        def sent_d(d, _):
+            t = lax.rem(w + d, nw)
+            rcopy(dbuf.at[t], r.at[0], ds.at[t], dr.at[0], sib).wait_send()
+            return 0
+
+        lax.fori_loop(1, nw, sent_d, 0)
+
+    rflat = r.reshape(place.shape[0], HD)
+    size = place.shape[0] // CHUNKS
     high = size - LOW
 
     def dev(axis, off):
@@ -470,15 +498,24 @@
         for base, b_off in ((4, 0), (8, -1), (12, 1), (16, 2)):
             hop(p, base + 2, b_off, 2, 1, sib).wait_recv()
             hop(p, base + 3, b_off, 2, 2, sib).wait_recv()
+        if p == 0:
+            for cp in local[9:15]:
+                cp.wait()
+        power = jnp.zeros((size, 1), F32)
+        for t in range(nn):
+            m = xs[t // NX, t % NX, lo : lo + size, :].astype(F32)
+            power = power + jnp.sum(m * m, axis=1, keepdims=True)
+        inv = lax.rsqrt(power / (nn * HD) + norm_eps)
         units = jnp.zeros((size, 4 * fw), F32)
         for t in range(nn):
-            units = units + mm(xs[t // NX, t % NX, lo : lo + size, :], wgt[t * HD : (t + 1) * HD, :])
+            m = xs[t // NX, t % NX, lo : lo + size, :].astype(F32)
+            m = (m * inv * expert_gain[:, t * HD : (t + 1) * HD]).astype(BF16)
+            units = units + mm(m, wgt[:, t * HD : (t + 1) * HD], DIMS1)
         gt = units[:, : 2 * fw]
         act = gt / (1.0 + jnp.exp(-gt)) * units[:, 2 * fw :]
         row = lax.rem(iota(act.shape, 0), 2 * CAP)
         keep = (row >= CAP) == (iota(act.shape, 1) >= fw)
         act = jnp.where(keep, act, 0.0).astype(BF16)
-        dn = down[...].reshape(2 * fw, -1)
         for t in range(nn):
             src[t // NX, t % NX, lo : lo + size, :] = mm(act, dn[:, t * HD : (t + 1) * HD]).astype(BF16)
         b2 = pos_of(axis, 2)
@@ -528,7 +565,7 @@
         t2[p, 1, LOW:, :] = (m2[p, bm, LOW:, :].astype(F32) + f2[p, LOW:, :].astype(F32)).astype(BF16)
         t2d(p, 1, dev(1 - axis, -1)).start()
 
-    bflat = bbuf.reshape(place.shape[1], HD)
+    bflat = bbuf.reshape(place.shape[0], HD)
 
     def stage8(p):
         j, axis = ORDER[p], p % 2
@@ -549,12 +586,31 @@
                 else:
                     rcopy(a, bk.at[w], es.at[rel * 2 + core], er.at[w], (t, n)).start()
 
+    def drain_pipe():
+        def sent_b(d, _):
+            t = lax.rem(nz + c + d, nw)
+            rcopy(bbuf.at[t], bk.at[w], es.at[t], er.at[w], sib).wait_send()
+            return 0
+
+        lax.fori_loop(1, nw, sent_b, 0)
+        for p in range(CHUNKS):
+            for slot in range(20):
+                half = 0 if slot < 2 or slot % 4 < 2 else slot % 4 - 1
+                hop(p, slot, 0, 0, half, sib).wait_send()
+            f1d(p, 0, 0, LOW, sib).wait_send()
+            f1d(p, 1, LOW, high, sib).wait_send()
+            f2d(p, 4, 0, LOW, sib).wait_send()
+            f2d(p, 5, LOW, high, sib).wait_send()
+            for k in range(2):
+                t1d(p, k, sib).wait_send()
+                t2d(p, k, sib).wait_send()
+
     stages = (stage0, stage1, stage2, stage3, stage4, stage5, stage6, stage7, stage8)
     for t in range(CHUNKS + len(stages) - 1):
         for k in reversed(range(len(stages))):
             if 0 <= t - k < CHUNKS:
                 stages[k](t - k)
-        if t == 0:
+        if t == 3:
             fill_router()
 
     def wait_b(d, _):
@@ -564,59 +620,16 @@
 
     lax.fori_loop(0, nw, wait_b, 0)
     moe = lax.dot_general(
-        mix[...], bk.reshape(place.shape[1], HD)[...].astype(F32), (((1,), (0,)), ((), ())),
+        mix[...], bk.reshape(place.shape[0], HD)[...].astype(F32), DIMS0,
         precision=lax.Precision.HIGHEST, preferred_element_type=F32,
     )
     layer_out[...] = (mx[n].astype(F32) + moe).astype(BF16)
 
-    for s in range(nz // 2):
-        for i in range(2):
-            if s < nz // 2 - 1 or i == 0:
-                ring(s, c if i == 0 else 1 - c).wait_send()
-        oring(s).wait_send()
-    side(z, c).wait_send()
-    o_side.wait_send()
-    for s in range(1, nz // 2):
-        for sub in range(2):
-            side(chip(-sg * s), sub).wait_send()
-        oside(s, True).wait_send()
-    side(chip(nz // 2), c).wait_send()
-    oside(nz // 2, True).wait_send()
-
-    def sent_w(d, _):
-        t = lax.rem(w + d, nw)
-        rcopy(ps.at[t], pr.at[w], pss.at[t], psr.at[w], sib).wait_send()
-        rcopy(dbuf.at[t], r.at[0], ds.at[t], dr.at[0], sib).wait_send()
-        return 0
-
-    lax.fori_loop(1, nw, sent_w, 0)
-
-    def sent_b(d, _):
-        t = lax.rem(nz + c + d, nw)
-        rcopy(bbuf.at[t], bk.at[w], es.at[t], er.at[w], sib).wait_send()
-        return 0
-
-    lax.fori_loop(1, nw, sent_b, 0)
-
-    def sent_n(d, _):
-        t = lax.rem(n + d, nn)
-        rcopy(part.at[t], rbuf.at[n], s1.at[t], r1s.at[n], sib).wait_send()
-        rcopy(ssb.at[n], ssb.at[n], s3.at[t], r3s.at[n], sib).wait_send()
-        rcopy(mx.at[n], mx.at[n], s2.at[t], r2s.at[n], sib).wait_send()
-        return 0
-
-    lax.fori_loop(1, nn, sent_n, 0)
-    for p in range(CHUNKS):
-        for slot in range(20):
-            half = 0 if slot < 2 or slot % 4 < 2 else slot % 4 - 1
-            hop(p, slot, 0, 0, half, sib).wait_send()
-        f1d(p, 0, 0, LOW, sib).wait_send()
-        f1d(p, 1, LOW, high, sib).wait_send()
-        f2d(p, 4, 0, LOW, sib).wait_send()
-        f2d(p, 5, LOW, high, sib).wait_send()
-        for k in range(2):
-            t1d(p, k, sib).wait_send()
-            t2d(p, k, sib).wait_send()
+    drain_ring()
+    drain_out()
+    drain_plane()
+    drain_dispatch()
+    drain_pipe()
 
 
 def body(
@@ -633,23 +646,27 @@
     cache = cache_keys.shape[1]
     vm = pl.BlockSpec(memory_space=pltpu.VMEM)
     sm = pl.BlockSpec(memory_space=pltpu.SMEM)
+    hbm = pl.BlockSpec(memory_space=pl.ANY)
     dma = pltpu.SemaphoreType.DMA
 
     def v(*shape, t=BF16):
         return pltpu.VMEM(shape, t)
 
     pair = rows // nw // 2
+    fw = gate_weight.shape[2]
     scratch = [
+        v(tok, width), v(E, width), v(4 * fw, width), v(2 * fw, width), v(cache, HD), v(cache, HD),
+        v(*prefix_keys.shape), v(*prefix_values.shape), v(tok, 3 * HD, t=F32),
         v(tok, width), v(nz, 2, 3, 64, HD), v(nz, 2, 64, HD), v(nw, 16, HD), v(nw, 16, HD),
         v(tok, HD), v(tok, HD), v(tok, HD), v(tok, cache, t=F32), v(tok, tok, t=F32), v(tok, tok, t=F32),
-        v(cache, tok), v(nn, tok, HD), v(nn, tok, HD), v(nn, tok, HD), v(nn, 8, HD, t=F32),
-        v(width, 4 * gate_weight.shape[2]), v(expert_ids.shape[1], tok, HD, t=jnp.int32), v(tok, rows), v(tok, rows, t=F32),
+        v(cache, tok), v(nn, tok, HD), v(nn, tok, HD), v(nn, tok, HD),
+        v(expert_ids.shape[1], tok, t=jnp.int32), v(rows, tok), v(rows, tok, t=F32),
         v(nw, pair, 2, HD), v(nw, pair, 2, HD), v(NY, NX, rows, HD), v(NY, NX, rows, HD),
         v(CHUNKS, 2, 4, size, HD), v(CHUNKS, 4, size, HD), v(CHUNKS, 2, 4, size, HD), v(CHUNKS, 4, size, HD),
         v(CHUNKS, 2, size, HD), v(CHUNKS, size, HD), v(CHUNKS, 2, size, HD), v(nw, pair, 2, HD), v(nw, pair, 2, HD),
-        dma((4,)), dma((nz // 2, 2)), dma((nz // 2, 2)), dma((nz, 2)), dma((nz, 2)),
+        dma((16,)), dma((nz // 2, 2)), dma((nz // 2, 2)), dma((nz, 2)), dma((nz, 2)),
         dma((nz // 2,)), dma((nz // 2,)), dma((nz + 1,)), dma((nz + 1,)), dma((nw,)), dma((nw,)),
-        dma((nn,)), dma((nn,)), dma((nn,)), dma((nn,)), dma((nn,)), dma((nn,)), dma((nw,)), dma((nw,)),
+        dma((nn,)), dma((nn,)), dma((nn,)), dma((nn,)), dma((nw,)), dma((nw,)),
         dma((CHUNKS, 20)), dma((CHUNKS, 20)), dma((CHUNKS, 8)), dma((CHUNKS, 8)), dma((nw,)), dma((nw,)),
     ]
     return pl.pallas_call(
@@ -659,7 +676,7 @@
             jax.ShapeDtypeStruct(cache_keys.shape, BF16),
             jax.ShapeDtypeStruct(cache_values.shape, BF16),
         ),
-        in_specs=[sm, sm] + [vm] * 18,
+        in_specs=[sm, sm] + [vm] * 5 + [hbm] * 13,
         out_specs=(vm, vm, vm),
         scratch_shapes=scratch,
         compiler_params=pltpu.CompilerParams(
@@ -667,9 +684,10 @@
         ),
         name="layer",
     )(
-        cache_lengths, accepted, hidden, attn_gain[None], expert_gain[None], query_weight, key_weight, value_weight,
-        output_weight, router_weight, gate_weight, up_weight, down_weight, prefix_keys, prefix_values,
-        cache_keys, cache_values, parents, group_ids[None], expert_ids,
+        cache_lengths, accepted, attn_gain[None], expert_gain[None], parents, group_ids[None], expert_ids.T,
+        hidden, query_weight, key_weight, value_weight, output_weight, router_weight.T,
+        jnp.swapaxes(gate_weight, 1, 2), jnp.swapaxes(up_weight, 1, 2), down_weight,
+        prefix_keys, prefix_values, cache_keys, cache_values,
     )
 
 

time: 167 us -> 135 us (0.81)
  Pallas kernels: 155 us -> 129 us
  local copies, waits for them, and re-layouts: 9.76 us -> 3.74 us
    pallas_call x1, Pallas kernels: 155 us -> 129 us  [body(): pl.pallas_call(layer_kernel, out_shape=(jax.ShapeDtypeStruct((tok, HD), B...]
    unnamed x13 -> x5, local copies, waits for them, and re-layouts: 9.76 us -> 3.74 us
where the time goes in v3:
time: 135 us
  Pallas kernels  129 us (96%)
  local copies, waits for them, and re-layouts  3.74 us (3%)
  between operations  1.94 us (1%)
    pallas_call x1, Pallas kernels, body(): pl.pallas_call(layer_kernel, out_shape=(jax.ShapeDtypeStruct((tok, HD), B...  129 us
    unnamed x5, local copies, waits for them, and re-layouts  3.74 us

profile of v3, /device:TPU:1, one launch (start us, length us, event | category | flops | bytes accessed | tf_op | source)
XLA Modules:
  0.0 135.0 jit_solution(16172517796966353101)
XLA Ops:
  1.9 129.3 %layer.1 = (bf16[64,128]{1,0:T(8,128)(2,1)}, bf16[1,1024,128]{2,1,0:T(8,128)(2,1)}, bf16[1,1024,128]{2,1,0:T(8,128)(2,1)}) custom-call(s32[1]{0:T(128)S(6)} %copy.26.lens, s32[1]{0:T(128)S(6)} %copy.27.acc_node, f32[1,2048]{1,0:T(1,128)} %bitcast.10, f32[1,2048]{1,0:T(1,128)} %bitcast.11, s32[1,64]{1,0:T(1,128)} %parents.1, s32[1,32]{1,0:T(1,128)} %bitcast.13, ...), custom_call_target="tpu_custom_call" | custom-call | tf_op jit(solution)/shard_map/layer/pallas_call | solution.py:672
  131.2 1.3 copy.28
  132.5 0.0 copy-start
  132.5 1.7 %copy.29 = bf16[1,1024,128]{2,1,0:T(8,128)(2,1)} copy(bf16[1,1024,128]{2,1,0:T(8,128)(2,1)} %get-tuple-element.7) | data formatting | bytes 524288
  134.3 0.0 copy-done
  134.3 0.7 copy.30
Async XLA Ops:
  132.5 1.7 %copy-start = (bf16[1,1024,128]{2,1,0:T(8,128)(2,1)S(1)}, bf16[1,1024,128]{2,1,0:T(8,128)(2,1)}, u32[]{:S(2)}) copy-start(bf16[1,1024,128]{2,1,0:T(8,128)(2,1)} %get-tuple-element.8) | copy-start | bytes 786436

commit v4 on v3

--- a/solution.py
+++ b/solution.py
@@ -120,11 +120,12 @@
     side(z, 1 - c).wait_recv()
     ring(0, 1 - c).start()
 
-    local[4].wait()
-    hv = hidden[...].astype(F32)
-    power = jnp.mean(hv * hv, axis=-1, keepdims=True)
-    normed[...] = (hv * lax.rsqrt(power + norm_eps) * attn_gain[...]).astype(BF16)
-    proj[...] = jnp.zeros_like(proj)
+    def fill_norm():
+        local[4].wait()
+        hv = hidden[...].astype(F32)
+        power = jnp.mean(hv * hv, axis=-1, keepdims=True)
+        normed[...] = (hv * lax.rsqrt(power + norm_eps) * attn_gain[...]).astype(BF16)
+        proj[...] = jnp.zeros_like(proj)
 
     def fill_prefix():
         local[5].wait()
@@ -198,44 +199,48 @@
             b = jnp.concatenate([g[k, 0, i], g[k, 1, i]], axis=0)
             proj[:, i * HD : (i + 1) * HD] += mm(a, b)
 
-    fill_prefix()
+    half = nz // 2
     rcopy(osib, osib, ofs.at[nz], ofr.at[nz], sib).wait_recv()
     oring(0).start()
     cp_own = pltpu.make_async_copy(ps.at[w], pr.at[w], psr.at[w])
-    cp_own.start()
-    rcopy(ps.at[sib_w], pr.at[w], pss.at[sib_w], psr.at[w], sib).start()
-    project(z)
-    fillers = {1: fill_tree, 2: fill_slots}
-    for s in range(1, nz // 2):
-        for i in range(2):
+
+    def seen(k):
+        for sub in range(2):
+            side(k, sub).wait_recv()
+
+    for s in range(1, half + 1):
+        for i in range(2 if s < half else 1):
             sub = c if i == 0 else 1 - c
             got(s - 1, sub).wait_recv()
-            if s < nz // 2 - 1 or i == 0:
+            if s < half - 1 or (s < half and i == 0):
                 ring(s, sub).start()
             side(chip(-sg * s), sub).start()
+        if s == 1:
+            fill_norm()
+        if s == 2:
+            fill_prefix()
+            cp_own.start()
+            rcopy(ps.at[sib_w], pr.at[w], pss.at[sib_w], psr.at[w], sib).start()
+            send_prefix(chip(-sg))
         ogot(s - 1).wait_recv()
-        oring(s).start()
+        if s < half:
+            oring(s).start()
         oside(s, True).start()
-        send_prefix(chip(-sg * s))
-        if s > 1:
-            for sub in range(2):
-                side(chip(sg * (s - 1)), sub).wait_recv()
+        if s >= 2:
+            if s < half:
+                send_prefix(chip(-sg * s))
+            seen(chip(sg * (s - 1)))
             send_prefix(chip(sg * (s - 1)))
             project(chip(sg * (s - 1)))
-        project(chip(-sg * s))
-        if s in fillers:
-            fillers[s]()
-    got(nz // 2 - 1, c).wait_recv()
-    side(chip(nz // 2), c).start()
-    ogot(nz // 2 - 1).wait_recv()
-    oside(nz // 2, True).start()
-    for sub in range(2):
-        side(chip(sg * (nz // 2 - 1)), sub).wait_recv()
-    send_prefix(chip(sg * (nz // 2 - 1)))
-    side(chip(nz // 2), 1 - c).wait_recv()
-    send_prefix(chip(nz // 2))
-    project(chip(sg * (nz // 2 - 1)))
-    project(chip(nz // 2))
+            project(chip(-sg * (s - 1)))
+        if s == 3:
+            project(z)
+            fill_tree()
+        if s == 4:
+            fill_slots()
+    side(chip(half), 1 - c).wait_recv()
+    send_prefix(chip(half))
+    project(chip(half))
     for i, ref in enumerate((qs, ks, vs)):
         ref[...] = proj[:, i * HD : (i + 1) * HD].astype(BF16)
 
@@ -606,11 +611,10 @@
                 t2d(p, k, sib).wait_send()
 
     stages = (stage0, stage1, stage2, stage3, stage4, stage5, stage6, stage7, stage8)
-    for t in range(CHUNKS + len(stages) - 1):
-        for k in reversed(range(len(stages))):
-            if 0 <= t - k < CHUNKS:
-                stages[k](t - k)
-        if t == 3:
+    for k in range(len(stages)):
+        for p in range(CHUNKS):
+            stages[k](p)
+        if k == 1:
             fill_router()
 
     def wait_b(d, _):

time: 135 us -> 127 us (0.941)
  Pallas kernels: 129 us -> 121 us
    pallas_call x1, Pallas kernels: 129 us -> 121 us  [body(): pl.pallas_call(layer_kernel, out_shape=(jax.ShapeDtypeStruct((tok, HD), B...]
where the time goes in v4:
time: 127 us
  Pallas kernels  121 us (95%)
  local copies, waits for them, and re-layouts  3.74 us (3%)
  between operations  1.94 us (2%)
    pallas_call x1, Pallas kernels, body(): pl.pallas_call(layer_kernel, out_shape=(jax.ShapeDtypeStruct((tok, HD), B...  121 us
    unnamed x5, local copies, waits for them, and re-layouts  3.74 us

profile of v4, /device:TPU:1, one launch (start us, length us, event | category | flops | bytes accessed | tf_op | source)
XLA Modules:
  0.0 126.7 jit_solution(14200440161330111305)
XLA Ops:
  1.9 121.0 %layer.1 = (bf16[64,128]{1,0:T(8,128)(2,1)}, bf16[1,1024,128]{2,1,0:T(8,128)(2,1)}, bf16[1,1024,128]{2,1,0:T(8,128)(2,1)}) custom-call(s32[1]{0:T(128)S(6)} %copy.26.lens, s32[1]{0:T(128)S(6)} %copy.27.acc_node, f32[1,2048]{1,0:T(1,128)} %bitcast.10, f32[1,2048]{1,0:T(1,128)} %bitcast.11, s32[1,64]{1,0:T(1,128)} %parents.1, s32[1,32]{1,0:T(1,128)} %bitcast.13, ...), custom_call_target="tpu_custom_call" | custom-call | tf_op jit(solution)/shard_map/layer/pallas_call | solution.py:676
  122.9 1.3 %copy.28 = bf16[64,128]{1,0:T(8,128)(2,1)} copy(bf16[64,128]{1,0:T(8,128)(2,1)} %get-tuple-element.6) | data formatting | bytes 32768
  124.2 0.0 copy-start
  124.2 1.7 %copy.29 = bf16[1,1024,128]{2,1,0:T(8,128)(2,1)} copy(bf16[1,1024,128]{2,1,0:T(8,128)(2,1)} %get-tuple-element.7) | data formatting | bytes 524288
  125.9 0.0 copy-done
  126.0 0.7 copy.30
Async XLA Ops:
  124.2 1.7 %copy-start = (bf16[1,1024,128]{2,1,0:T(8,128)(2,1)S(1)}, bf16[1,1024,128]{2,1,0:T(8,128)(2,1)}, u32[]{:S(2)}) copy-start(bf16[1,1024,128]{2,1,0:T(8,128)(2,1)} %get-tuple-element.8) | copy-start | bytes 786436

commit v5 on v4

--- a/solution.py
+++ b/solution.py
@@ -55,7 +55,7 @@
     layer_out, new_k, new_v,
     hidden, router, wgt, dn, cache_k, cache_v, pk, pv, proj,
     normed, g, go, ps, pr, qs, ks, vs, cs, ts, anc, put, part, rbuf, mx, tgt, place, mix,
-    dbuf, r, xs, src, r1, f1, t1, m2, r2, f2, t2, bbuf, bk,
+    dbuf, r, xs, src, r1, f1, t1, m2, r2, bbuf, bk,
     ls, rs, rr, fs, fr, os, orr, ofs, ofr, pss, psr, s1, r1s, s2, r2s, ds, dr, ss, rrs, us, ur, es, er,
 ):
     nz, nn, nw = g.shape[0], part.shape[0], pr.shape[0]
@@ -360,20 +360,17 @@
     cp_d = pltpu.make_async_copy(dbuf.at[w], r.at[nz + c], dr.at[nz + c])
     cp_d.start()
     send_d(0, 1 - c)
-    for k in range(1, nz // 2):
-        for dz in (k, -k):
-            for core in range(2):
-                send_d(dz, core)
-    for core in range(2):
-        send_d(nz // 2, core)
+    for dz in (1, -1, 2, -2, 3, -3, 4):
+        for core in range(2):
+            send_d(dz, core)
+    for dz in (nz // 2, -7, 7, -6, 6, -5, 5, -4):
+        for core in range(2):
+            send_d(dz, core)
+
     def send2(d, _):
         t = lax.rem(n + d, nn)
         rcopy(mx.at[n], mx.at[n], s2.at[t], r2s.at[n], (w, t)).start()
         return 0
-
-    lax.fori_loop(1, nn, send2, 0)
-    compact(ks, cache_k, new_k)
-    compact(vs, cache_v, new_v)
 
     def wait2(d, _):
         t = lax.rem(n + d, nn)
@@ -451,14 +448,14 @@
         xs[y, x, pl.ds(j * size, size), :] = rflat[pl.ds(j * size, size), :]
         hop(p, 0, 0, 0, 0, dev(axis, 1)).start()
         hop(p, 1, 0, 0, 0, dev(axis, -1)).start()
+        hop(p, 2, 0, 0, 0, dev(axis, 2)).start()
         hop(p, 4, 0, 0, 0, dev(1 - axis, 1)).start()
         hop(p, 5, 0, 0, 0, dev(1 - axis, -1)).start()
 
     def stage1(p):
         axis = p % 2
-        for slot, off, half in ((0, -1, 1), (1, 1, 2)):
+        for slot, off in ((0, -1), (1, 1)):
             hop(p, slot, off, 0, 0, sib).wait_recv()
-            hop(p, slot + 2, off, 0, half, dev(axis, -off)).start()
             hop(p, 8 + 4 * slot, off, 0, 0, dev(1 - axis, 1)).start()
             hop(p, 9 + 4 * slot, off, 0, 0, dev(1 - axis, -1)).start()
 
@@ -472,8 +469,7 @@
     def stage2(p):
         axis = p % 2
         second(p, 4, 0)
-        hop(p, 2, 2, 0, 1, sib).wait_recv()
-        hop(p, 3, 2, 0, 2, sib).wait_recv()
+        hop(p, 2, 2, 0, 0, sib).wait_recv()
         hop(p, 16, 2, 0, 0, dev(1 - axis, 1)).start()
         hop(p, 17, 2, 0, 0, dev(1 - axis, -1)).start()
         second(p, 8, -1)
@@ -492,10 +488,6 @@
 
     def f1d(p, slot, lo, ln, to):
         ref = f1.at[p, :, pl.ds(lo, ln), :]
-        return rcopy(ref, ref, us.at[p, slot], ur.at[p, slot], to)
-
-    def f2d(p, slot, lo, ln, to):
-        ref = f2.at[p, pl.ds(lo, ln), :]
         return rcopy(ref, ref, us.at[p, slot], ur.at[p, slot], to)
 
     def stage4(p):
@@ -532,8 +524,8 @@
     def t1d(p, k, to):
         return rcopy(t1.at[p, k], r1.at[p, k], us.at[p, 2 + k], ur.at[p, 2 + k], to)
 
-    def t2d(p, k, to):
-        return rcopy(t2.at[p, k], r2.at[p, k], us.at[p, 6 + k], ur.at[p, 6 + k], to)
+    def last(p, k, b, to):
+        return rcopy(m2.at[p, b], r2.at[p, k], us.at[p, 4 + k], ur.at[p, 4 + k], to)
 
     def stage5(p):
         axis, lo = p % 2, ORDER[p] * size
@@ -552,32 +544,18 @@
         t1d(p, 0, sib).wait_recv()
         t1d(p, 1, sib).wait_recv()
         m2[p] = (val(axis, pos_of(axis, 0), lo, size) + r1[p, 0].astype(F32) + r1[p, 1].astype(F32)).astype(BF16)
-        b2 = pos_of(1 - axis, 2)
-        rcopy(m2.at[p, b2, pl.ds(0, LOW), :], f2.at[p, pl.ds(0, LOW), :], us.at[p, 4], ur.at[p, 4], dev(1 - axis, 1)).start()
-        rcopy(
-            m2.at[p, b2, pl.ds(LOW, high), :], f2.at[p, pl.ds(LOW, high), :], us.at[p, 5], ur.at[p, 5], dev(1 - axis, -1)
-        ).start()
-
-    def stage7(p):
-        axis = p % 2
-        bp, bm = pos_of(1 - axis, 1), pos_of(1 - axis, -1)
-        t2[p, 0, LOW:, :] = m2[p, bp, LOW:, :]
-        t2[p, 1, :LOW, :] = m2[p, bm, :LOW, :]
-        f2d(p, 4, 0, LOW, sib).wait_recv()
-        t2[p, 0, :LOW, :] = (m2[p, bp, :LOW, :].astype(F32) + f2[p, :LOW, :].astype(F32)).astype(BF16)
-        t2d(p, 0, dev(1 - axis, 1)).start()
-        f2d(p, 5, LOW, high, sib).wait_recv()
-        t2[p, 1, LOW:, :] = (m2[p, bm, LOW:, :].astype(F32) + f2[p, LOW:, :].astype(F32)).astype(BF16)
-        t2d(p, 1, dev(1 - axis, -1)).start()
+        for k, off in enumerate((1, -1, 2)):
+            last(p, k, pos_of(1 - axis, off), dev(1 - axis, off)).start()
 
     bflat = bbuf.reshape(place.shape[0], HD)
 
     def stage8(p):
         j, axis = ORDER[p], p % 2
-        t2d(p, 0, sib).wait_recv()
-        t2d(p, 1, sib).wait_recv()
+        for k in range(3):
+            last(p, k, 0, sib).wait_recv()
         bflat[pl.ds(j * size, size), :] = (
-            m2[p, pos_of(1 - axis, 0)].astype(F32) + r2[p, 0].astype(F32) + r2[p, 1].astype(F32)
+            (m2[p, pos_of(1 - axis, 0)].astype(F32) + r2[p, 0].astype(F32))
+            + (r2[p, 1].astype(F32) + r2[p, 2].astype(F32))
         ).astype(BF16)
         for i in range(nz // CHUNKS):
             rel = j * (nz // CHUNKS) + i
@@ -600,22 +578,27 @@
         lax.fori_loop(1, nw, sent_b, 0)
         for p in range(CHUNKS):
             for slot in range(20):
-                half = 0 if slot < 2 or slot % 4 < 2 else slot % 4 - 1
+                if slot == 3:
+                    continue
+                half = 0 if slot < 3 or slot % 4 < 2 else slot % 4 - 1
                 hop(p, slot, 0, 0, half, sib).wait_send()
             f1d(p, 0, 0, LOW, sib).wait_send()
             f1d(p, 1, LOW, high, sib).wait_send()
-            f2d(p, 4, 0, LOW, sib).wait_send()
-            f2d(p, 5, LOW, high, sib).wait_send()
             for k in range(2):
                 t1d(p, k, sib).wait_send()
-                t2d(p, k, sib).wait_send()
-
-    stages = (stage0, stage1, stage2, stage3, stage4, stage5, stage6, stage7, stage8)
+            for k in range(3):
+                last(p, k, 0, sib).wait_send()
+
+    stages = (stage0, stage1, stage2, stage3, stage4, stage5, stage6, stage8)
     for k in range(len(stages)):
         for p in range(CHUNKS):
             stages[k](p)
-        if k == 1:
-            fill_router()
+        if k == 4:
+            compact(ks, cache_k, new_k)
+            compact(vs, cache_v, new_v)
+        if k == 6:
+            lax.fori_loop(1, nn, send2, 0)
+    fill_router()
 
     def wait_b(d, _):
         t = lax.rem(w + d, nw)
@@ -667,7 +650,7 @@
         v(expert_ids.shape[1], tok, t=jnp.int32), v(rows, tok), v(rows, tok, t=F32),
         v(nw, pair, 2, HD), v(nw, pair, 2, HD), v(NY, NX, rows, HD), v(NY, NX, rows, HD),
         v(CHUNKS, 2, 4, size, HD), v(CHUNKS, 4, size, HD), v(CHUNKS, 2, 4, size, HD), v(CHUNKS, 4, size, HD),
-        v(CHUNKS, 2, size, HD), v(CHUNKS, size, HD), v(CHUNKS, 2, size, HD), v(nw, pair, 2, HD), v(nw, pair, 2, HD),
+        v(CHUNKS, 3, size, HD), v(nw, pair, 2, HD), v(nw, pair, 2, HD),
         dma((16,)), dma((nz // 2, 2)), dma((nz // 2, 2)), dma((nz, 2)), dma((nz, 2)),
         dma((nz // 2,)), dma((nz // 2,)), dma((nz + 1,)), dma((nz + 1,)), dma((nw,)), dma((nw,)),
         dma((nn,)), dma((nn,)), dma((nn,)), dma((nn,)), dma((nw,)), dma((nw,)),

time: 127 us -> 126 us (level)
  no operation moved by 1% of the time
where the time goes in v5:
time: 126 us
  Pallas kernels  120 us (95%)
  local copies, waits for them, and re-layouts  3.74 us (3%)
  between operations  1.94 us (2%)
    pallas_call x1, Pallas kernels, body(): pl.pallas_call(layer_kernel, out_shape=(jax.ShapeDtypeStruct((tok, HD), B...  120 us
    unnamed x5, local copies, waits for them, and re-layouts  3.74 us

profile of v5, /device:TPU:1, one launch (start us, length us, event | category | flops | bytes accessed | tf_op | source)
XLA Modules:
  0.0 125.9 jit_solution(221516868193769927)
XLA Ops:
  1.9 120.2 %layer.1 = (bf16[64,128]{1,0:T(8,128)(2,1)}, bf16[1,1024,128]{2,1,0:T(8,128)(2,1)}, bf16[1,1024,128]{2,1,0:T(8,128)(2,1)}) custom-call(s32[1]{0:T(128)S(6)} %copy.26.lens, s32[1]{0:T(128)S(6)} %copy.27.acc_node, f32[1,2048]{1,0:T(1,128)} %bitcast.10, f32[1,2048]{1,0:T(1,128)} %bitcast.11, s32[1,64]{1,0:T(1,128)} %parents.1, s32[1,32]{1,0:T(1,128)} %bitcast.13, ...), custom_call_target="tpu_custom_call" | custom-call | tf_op jit(solution)/shard_map/layer/pallas_call | solution.py:659
  122.1 1.3 %copy.28 = bf16[64,128]{1,0:T(8,128)(2,1)} copy(bf16[64,128]{1,0:T(8,128)(2,1)} %get-tuple-element.6) | data formatting | bytes 32768
  123.4 0.0 copy-start
  123.4 1.7 %copy.29 = bf16[1,1024,128]{2,1,0:T(8,128)(2,1)} copy(bf16[1,1024,128]{2,1,0:T(8,128)(2,1)} %get-tuple-element.7) | data formatting | bytes 524288
  125.1 0.0 copy-done
  125.1 0.7 copy.30
Async XLA Ops:
  123.4 1.7 %copy-start = (bf16[1,1024,128]{2,1,0:T(8,128)(2,1)S(1)}, bf16[1,1024,128]{2,1,0:T(8,128)(2,1)}, u32[]{:S(2)}) copy-start(bf16[1,1024,128]{2,1,0:T(8,128)(2,1)} %get-tuple-element.8) | copy-start | bytes 786436

commit v6 on v5

--- a/solution.py
+++ b/solution.py
@@ -366,6 +366,8 @@
     for dz in (nz // 2, -7, 7, -6, 6, -5, 5, -4):
         for core in range(2):
             send_d(dz, core)
+    compact(ks, cache_k, new_k)
+    compact(vs, cache_v, new_v)
 
     def send2(d, _):
         t = lax.rem(n + d, nn)
@@ -593,9 +595,6 @@
     for k in range(len(stages)):
         for p in range(CHUNKS):
             stages[k](p)
-        if k == 4:
-            compact(ks, cache_k, new_k)
-            compact(vs, cache_v, new_v)
         if k == 6:
             lax.fori_loop(1, nn, send2, 0)
     fill_router()

time: 126 us -> 125 us (level)
  no operation moved by 1% of the time
where the time goes in v6:
time: 125 us
  Pallas kernels  119 us (95%)
  local copies, waits for them, and re-layouts  3.74 us (3%)
  between operations  1.94 us (2%)
    pallas_call x1, Pallas kernels, body(): pl.pallas_call(layer_kernel, out_shape=(jax.ShapeDtypeStruct((tok, HD), B...  119 us
    unnamed x5, local copies, waits for them, and re-layouts  3.74 us

profile of v6, /device:TPU:1, one launch (start us, length us, event | category | flops | bytes accessed | tf_op | source)
XLA Modules:
  0.0 124.7 jit_solution(2110072922928591951)
XLA Ops:
  1.9 119.0 %layer.1 = (bf16[64,128]{1,0:T(8,128)(2,1)}, bf16[1,1024,128]{2,1,0:T(8,128)(2,1)}, bf16[1,1024,128]{2,1,0:T(8,128)(2,1)}) custom-call(s32[1]{0:T(128)S(6)} %copy.26.lens, s32[1]{0:T(128)S(6)} %copy.27.acc_node, f32[1,2048]{1,0:T(1,128)} %bitcast.10, f32[1,2048]{1,0:T(1,128)} %bitcast.11, s32[1,64]{1,0:T(1,128)} %parents.1, s32[1,32]{1,0:T(1,128)} %bitcast.13, ...), custom_call_target="tpu_custom_call" | custom-call | tf_op jit(solution)/shard_map/layer/pallas_call | solution.py:658
  120.9 1.3 %copy.28 = bf16[64,128]{1,0:T(8,128)(2,1)} copy(bf16[64,128]{1,0:T(8,128)(2,1)} %get-tuple-element.6) | data formatting | bytes 32768
  122.2 0.0 copy-start
  122.2 1.7 %copy.29 = bf16[1,1024,128]{2,1,0:T(8,128)(2,1)} copy(bf16[1,1024,128]{2,1,0:T(8,128)(2,1)} %get-tuple-element.7) | data formatting | bytes 524288
  124.0 0.0 copy-done
  124.0 0.7 copy.30
Async XLA Ops:
  122.2 1.7 %copy-start = (bf16[1,1024,128]{2,1,0:T(8,128)(2,1)S(1)}, bf16[1,1024,128]{2,1,0:T(8,128)(2,1)}, u32[]{:S(2)}) copy-start(bf16[1,1024,128]{2,1,0:T(8,128)(2,1)} %get-tuple-element.8) | copy-start | bytes 786436
